TPU v7x, 128 devices: a whole 4x4x4 slice. The times are simulated.
128 devices in a mesh: grp: 2 (over core), band: 64 (over y, x, z).
Axes of the slice: x: 4, y: 4, z: 4, core: 2. Of those that a mesh axis runs over, the one named last changes fastest.
Arguments:
- fields: bfloat16 [2, 256, 640, 1280], P(None, None, ('grp', 'band')), may hold values from -4 to 4
- wave_order: int32 [640], replicated, may hold values from 0 to 639, as said below
- basis: bfloat16 [320, 2, 640, 641], P('band'), as said below
Outputs:
- whitened: bfloat16 [2, 320, 2, 641, 256], P('grp', 'band')
- factor: float32 [256, 256], replicated
Inputs may be any that keep to these rules, and one draw needn't show every extreme that they name: wave_order names every wavenumber once; slots 2 k and 2 k + 1 hold m and 639 - m for some m, in either order. With a = wave_order[2 k], b = wave_order[2 k + 1], colatitude theta_i = pi (i + 1/2) / 640, mu_i = cos(theta_i) and weight_i = (pi / 640) sin(theta_i): basis[k, 0, i, j] = weight_i P(a + j, a) and basis[k, 1, i, j] = weight_i P(j - 1, b), rounded to bfloat16, where P(m, m) = exp(m log(sin theta_i) + (lgamma(m + 3/2) - lgamma(m + 1) - lgamma(3/2)) / 2), P(m + 1, m) = sqrt(2 m + 3) mu_i P(m, m), P(n, m) = sqrt((4 n^2 - 1) / (n^2 - m^2)) (mu_i P(n - 1, m) - sqrt(((n - 1)^2 - m^2) / (4 (n - 1)^2 - 1)) P(n - 2, m)), and P(n, m) = 0 for n < m or n >= 640.
All inputs are finite; a program needn't handle non-finite values.
Results may differ from a plain program's by a relative error of at most 0.012.
The roundings to bfloat16 on the way count: a program that leaves them out, or rounds other values in their place, can miss the bound.
Values may be sent and summed in bfloat16 or wider, within the bound.
No kernel may reach another device: no remote copies, remote signals or barrier semaphores. Data moves between devices by JAX's collectives and lax.ppermute only.
A program may use at most 128 MiB of HBM per device.

v0:
```python
import math

import jax
import jax.numpy as jnp
from jax import lax
from jax.sharding import PartitionSpec as P


def fourier_table(wave_order, lon_count):
    lon_index = jnp.arange(lon_count, dtype=jnp.int32)
    phase = lon_index[:, None] * wave_order[None, :] % lon_count
    angle_grid = phase.astype(jnp.float32) * (2.0 * math.pi / lon_count)
    stacked = jnp.stack([jnp.cos(angle_grid), -jnp.sin(angle_grid)], axis=2)
    return stacked.reshape(lon_count, -1).astype(jnp.bfloat16)


def project(received, legendre):
    pair_count = legendre.shape[0]
    shaped = received.reshape(
        received.shape[0], received.shape[1], received.shape[2], pair_count, 2, 2
    )
    return jnp.einsum("ltaqhc,qhaj->lqcjt", shaped, legendre, preferred_element_type=jnp.float32)


def shards(fields, wave_order, basis):
    level_count, time_count, lat_rows, lon_count = fields.shape
    groups = lax.axis_size("grp")
    band_count = lax.axis_size("band")
    fourier = fourier_table(wave_order, lon_count)
    spectra = jnp.dot(fields.reshape(-1, lon_count), fourier, preferred_element_type=jnp.float32)
    spectra = spectra.astype(jnp.bfloat16).reshape(level_count, time_count, lat_rows, lon_count)
    group_index = lax.axis_index("grp")
    group_rows = lat_rows * band_count
    legendre = lax.dynamic_slice_in_dim(basis, group_index * group_rows, group_rows, 2)
    partial_value = project(
        lax.all_to_all(spectra, "band", split_axis=3, concat_axis=2, tiled=True), legendre
    )
    coefficients = lax.psum_scatter(partial_value, "grp", scatter_dimension=0, tiled=True)
    matrix = coefficients.reshape(-1, time_count)
    local_gram = lax.dot_general(
        matrix,
        matrix,
        (((0,), (0,)), ((), ())),
        precision=lax.Precision.HIGHEST,
        preferred_element_type=jnp.float32,
    )
    total_rows = matrix.shape[0] * groups * band_count
    gram_matrix = lax.psum(local_gram, ("grp", "band")) / total_rows
    lower_factor = jnp.linalg.cholesky(gram_matrix)
    inverse = jax.scipy.linalg.solve_triangular(
        lower_factor, jnp.eye(time_count, dtype=jnp.float32), lower=True
    )
    whitened = jnp.dot(
        matrix, inverse.T, precision=lax.Precision.HIGHEST, preferred_element_type=jnp.float32
    ).astype(jnp.bfloat16)
    return (whitened.reshape(coefficients.shape), lower_factor.T)


def solution(mesh):
    placed = (P(None, None, ("grp", "band"), None), P(), P("band", None, None, None))
    return jax.shard_map(
        shards,
        mesh=mesh,
        in_specs=placed,
        out_specs=(P("grp", "band", None, None, None), P()),
        check_vma=False,
    )
```

profile of v0, /device:TPU:1, one launch (start us, length us, event | category | flops | bytes accessed | tf_op | source)
XLA Modules:
  0.0 550.1 jit_solution(8592170329960440457)
XLA Ops:
  7.2 14.6 %cosine_convert_fusion = (bf16[1280,640,1]{1,0,2:T(8,128)(2,1)S(1)}, bf16[1280,640,1]{1,0,2:T(8,128)(2,1)S(1)}) fusion(s32[640]{0:T(1024)} %param.4), kind=kLoop, calls=%fused_computation.15 | loop fusion | flops 9830400 | bytes 3279360 | tf_op jit(solution)/shard_map/convert.1
  21.8 0.3 pad_maximum_fusion
  22.1 7.3 %copy.45 = bf16[1280,640,2]{0,2,1:T(2,128)(2,1)} copy(bf16[1280,640,2]{1,0,2:T(8,128)(2,1)S(1)} %pad_maximum_fusion) | data formatting | bytes 6553600 | tf_op jit(solution)/shard_map/stack | solution.py:13
  29.4 6.6 %convert_element_type.35 = bf16[1280,1280]{0,1:T(8,128)(2,1)S(1)} reshape(bf16[1280,640,2]{0,2,1:T(2,128)(2,1)} %copy.45) | data formatting | bytes 6553600 | tf_op jit(solution)/shard_map/convert_element_type | solution.py:14
  36.1 11.1 %copy.46 = bf16[2,256,5,1280]{3,2,1,0:T(8,128)(2,1)} copy(bf16[2,256,5,1280]{3,1,2,0:T(8,128)(2,1)} %param.3) | data formatting | bytes 13107200 | tf_op args[0]
  47.1 13.0 %reshape.132 = bf16[2560,1280]{1,0:T(8,128)(2,1)} reshape(bf16[2,256,5,1280]{3,2,1,0:T(8,128)(2,1)} %copy.46) | data formatting | bytes 13107200 | tf_op jit(solution)/shard_map/reshape | solution.py:30
  60.1 13.3 %fusion = bf16[2560,1280]{0,1:T(8,128)(2,1)} fusion(bf16[1280,1280]{0,1:T(8,128)(2,1)S(1)} %convert_element_type.35, bf16[2560,1280]{1,0:T(8,128)(2,1)} %reshape.132), kind=kOutput, calls=%fused_computation.3 | convolution fusion | flops 8391884800 | bytes 16384000 | tf_op jit(solution)/shard_map/dot_general | solution.py:30
  73.4 9.5 %copy.47 = bf16[2560,1280]{1,0:T(8,128)(2,1)} copy(bf16[2560,1280]{0,1:T(8,128)(2,1)} %fusion) | data formatting | bytes 13107200 | tf_op jit(solution)/shard_map/convert_element_type | solution.py:31
  82.9 12.7 %reshape.133 = bf16[2,256,5,1280]{3,2,1,0:T(8,128)(2,1)} reshape(bf16[2560,1280]{1,0:T(8,128)(2,1)} %copy.47) | data formatting | bytes 13107200 | tf_op jit(solution)/shard_map/reshape | solution.py:31
  95.6 17.0 %copy.48 = bf16[2,256,5,1280]{1,0,2,3:T(2,128)(2,1)} copy(bf16[2,256,5,1280]{3,2,1,0:T(8,128)(2,1)} %reshape.133) | data formatting | bytes 13107200 | tf_op jit(solution)/shard_map/reshape | solution.py:31
  112.6 12.2 %all-to-all-start = ((bf16[2,256,5,1280]{1,0,2,3:T(2,128)(2,1)}), bf16[2,256,5,1280]{1,0,2,3:T(2,128)(2,1)}, u32[]{:S(2)}, u32[]{:S(2)}) async-start(bf16[2,256,5,1280]{1,0,2,3:T(2,128)(2,1)} %copy.48), calls=%async_computation | async-start | bytes 13107200 | tf_op jit(solution)/shard_map/all_to_all | solution.py:36
  124.8 0.3 all-reduce.7.cloned.1.call-start
  125.1 15.5 %constant_dynamic-slice_fusion.2 = bf16[5,2,320,641]{2,1,3,0:T(2,128)(2,1)} fusion(bf16[5,2,640,641]{2,1,3,0:T(2,128)(2,1)} %param.5, s32[]{:T(128)S(6)} %select_n.25), kind=kLoop, calls=%fused_computation.54 | loop fusion | bytes 8204804 | tf_op jit(solution)/shard_map/dynamic_slice | solution.py:34
  140.6 17.6 %copy.65 = bf16[5,2,320,641]{3,2,1,0:T(8,128)(2,1)} copy(bf16[5,2,320,641]{2,1,3,0:T(2,128)(2,1)} %constant_dynamic-slice_fusion.2) | data formatting | bytes 8204800
  158.3 49.1 %all-to-all-done = bf16[2,256,5,1280]{1,0,2,3:T(2,128)(2,1)} async-done(((bf16[2,256,5,1280]{1,0,2,3:T(2,128)(2,1)}), bf16[2,256,5,1280]{1,0,2,3:T(2,128)(2,1)}, u32[]{:S(2)}, u32[]{:S(2)}) %all-to-all-start) | async-done | bytes 6553632 | tf_op jit(solution)/shard_map/all_to_all | solution.py:36
  207.4 6.8 %copy.50 = bf16[2,256,64,5,20]{1,0,4,3,2:T(2,128)(2,1)} copy(bf16[2,256,64,5,20]{1,0,3,4,2:T(2,128)(2,1)} %bitcast.5) | data formatting | bytes 13107200 | tf_op jit(solution)/shard_map/all_to_all | solution.py:36
  214.2 9.0 %convolution_bitcast_fusion = f32[2,5,2,641,256]{4,3,2,0,1:T(8,128)S(1)} fusion(bf16[2,256,320,5,2,2]{1,0,5,4,3,2:T(2,128)(2,1)} %bitcast.59, bf16[5,2,320,641]{3,2,1,0:T(8,128)(2,1)} %copy.65), kind=kOutput, calls=%fused_computation.5 | convolution fusion | flops 4200857600 | bytes 23783680 | tf_op jit(solution)/shard_map/ltaqhc,qhaj->lqcjt/dot_general | solution.py:22
  223.2 9.0 %copy.52 = f32[2,5,2,641,256]{4,2,3,1,0:T(2,128)} copy(f32[2,5,2,641,256]{4,3,2,0,1:T(8,128)S(1)} %convolution_bitcast_fusion) | data formatting | bytes 26255360 | tf_op jit(solution)/shard_map/ltaqhc,qhaj->lqcjt/transpose | solution.py:22
  232.3 0.6 copy-done
  232.9 0.6 dynamic-slice.3
  233.6 58.9 %all-reduce.7.cloned.1.call-done = f32[2,5,2,641,256]{4,2,3,1,0:T(2,128)} async-done(((f32[2,5,2,641,256]{4,2,3,1,0:T(2,128)}), f32[2,5,2,641,256]{4,2,3,1,0:T(2,128)}) %all-reduce.7.cloned.1.call-update) | async-done | bytes 13127696
  292.4 8.4 %fusion.35 = f32[5,2,641,256]{3,1,2,0:T(2,128)} fusion(f32[2,5,2,641,256]{4,2,3,1,0:T(2,128)} %all-reduce.7.cloned.1.call-done, u32[]{:T(128)} %bitcast.23), kind=kLoop, calls=%fused_computation.57 | loop fusion | bytes 13127684 | tf_op jit(solution)/shard_map/reshape.45
  300.8 17.8 %fusion.10 = f32[256,256]{0,1:T(8,128)} fusion(f32[5,2,641,256]{3,1,2,0:T(2,128)} %fusion.35), kind=kOutput, calls=%fused_computation.20 | convolution fusion | flops 5041029120 | bytes 6825984 | tf_op jit(solution)/shard_map/dot_general | solution.py:40
  318.6 8.4 %constant_dynamic-slice_fusion.1 = f32[1,5,2,641,256]{4,2,3,1,0:T(2,128)} fusion(f32[2,5,2,641,256]{4,2,3,1,0:T(2,128)} %all-reduce.7.cloned.1.call-done, u32[]{:T(128)} %bitcast.23), kind=kLoop, calls=%fused_computation.50 | loop fusion | bytes 13127684
  327.0 6.4 %copy.53 = f32[1,5,2,641,256]{4,3,2,1,0:T(8,128)} copy(f32[1,5,2,641,256]{4,2,3,1,0:T(2,128)} %constant_dynamic-slice_fusion.1) | data formatting | bytes 13127680 | tf_op jit(solution)/shard_map/reduce_scatter | solution.py:38
  333.4 8.4 %reshape.135 = f32[6410,256]{1,0:T(8,128)} reshape(f32[1,5,2,641,256]{4,3,2,1,0:T(8,128)} %copy.53) | data formatting | bytes 13127680 | tf_op jit(solution)/shard_map/reshape | solution.py:39
  341.8 121.0 %all-reduce.5.cloned.1.call-done = f32[256,256]{0,1:T(8,128)} async-done(((f32[256,256]{0,1:T(8,128)}), f32[256,256]{0,1:T(8,128)}) %all-reduce.5.cloned.1.call-update) | async-done | bytes 262160 | tf_op jit(solution)/shard_map/psum | solution.py:48
  462.8 1.0 broadcast_multiply_fusion
  463.9 1.0 fusion.16
  464.9 11.7 %cholesky.50 = f32[128,128]{1,0:T(8,128)S(1)} custom-call(f32[128,128]{1,0:T(8,128)S(1)} %cholesky.118), custom_call_target="Cholesky" | custom-call | tf_op jit(solution)/shard_map/jit(cholesky)/cholesky | solution.py:49
  476.7 9.8 %custom-call.15 = f32[1,128,128]{1,2,0:T(8,128)S(1)} custom-call(f32[1,128,128]{2,1,0:T(8,128)S(1)} %get-tuple-element.35), custom_call_target="InvertDiagBlocksLowerTriangular" | custom-call | tf_op jit(solution)/shard_map/jit(cholesky)/cholesky | solution.py:49
  486.5 0.2 constant_dynamic-update-slice_fusion.1
  486.7 0.3 convolution_subtract_fusion.1
  487.0 11.7 %cholesky.105 = f32[128,128]{1,0:T(8,128)S(1)} custom-call(f32[128,128]{1,0:T(8,128)S(1)} %convolution_subtract_fusion.1), custom_call_target="Cholesky" | custom-call | tf_op jit(solution)/shard_map/jit(cholesky)/cholesky | solution.py:49
  498.8 0.7 compare_reduce_fusion
  500.9 4.1 while.1
  501.0 0.6 fusion.37
  501.6 1.4 bitcast_dynamic-update-slice_fusion.2
  503.0 0.6 fusion.37
  503.6 1.4 bitcast_dynamic-update-slice_fusion.2
  505.0 19.9 %custom-call.16 = f32[2,128,128]{1,2,0:T(8,128)S(1)} custom-call(f32[2,128,128]{2,1,0:T(8,128)S(1)} %get-tuple-element.9), custom_call_target="InvertDiagBlocksLowerTriangular" | custom-call | tf_op jit(solution)/shard_map/jit(_solve_triangular)/triangular_solve | solution.py:50
  525.0 0.3 fusion.19
  525.3 0.3 convolution_subtract_fusion
  525.5 0.3 fusion.22
  525.8 7.5 %convolution_convert_fusion.1 = bf16[6410,256]{1,0:T(8,128)(2,1)S(1)} fusion(f32[6410,256]{1,0:T(8,128)} %reshape.135, f32[128,256]{1,0:T(8,128)S(1)} %fusion.22, f32[128,256]{1,0:T(8,128)S(1)} %fusion.19), kind=kOutput, calls=%fused_computation.4 | convolution fusion | flops 5042735616 | bytes 10107904 | tf_op jit(solution)/shard_map/dot_general | solution.py:53
  533.3 2.5 reshape.137
  535.8 6.2 %copy.58 = bf16[1,5,2,641,256]{4,2,3,1,0:T(2,128)(2,1)} copy(bf16[1,5,2,641,256]{4,3,2,1,0:T(8,128)(2,1)} %reshape.137) | data formatting | bytes 6563840
  542.0 0.8 copy.59
  (16 shorter events, 0.5 us)
Async XLA Ops:
  112.6 94.7 %all-to-all-start = ((bf16[2,256,5,1280]{1,0,2,3:T(2,128)(2,1)}), bf16[2,256,5,1280]{1,0,2,3:T(2,128)(2,1)}, u32[]{:S(2)}, u32[]{:S(2)}) async-start(bf16[2,256,5,1280]{1,0,2,3:T(2,128)(2,1)} %copy.48), calls=%async_computation | async-start | bytes 13107200 | tf_op jit(solution)/shard_map/all_to_all | solution.py:36
  124.8 167.6 %all-reduce.7.cloned.1.call-start = ((), (), s32[]{:S(2)}) async-start(), calls=%async_computation.2 | async-start | bytes 26255360
  232.2 0.7 copy-start
  232.3 230.6 %all-reduce.5.cloned.1.call-start = ((), (), s32[]{:S(2)}) async-start(), calls=%async_computation.1 | async-start | bytes 524288 | tf_op jit(solution)/shard_map/psum | solution.py:48
Sparse Core Ops, SparseCore 0:
  232.4 59.9 all-reduce.6
  318.7 144.0 all-reduce.4
where the time goes:
time: 561 us; the launch traced here: 550 us
  waiting for transfers between devices  229 us (41%)
  local copies, waits for them, and re-layouts  173 us (31%)
  other arithmetic  70.9 us (13%)
  matrix products  48.9 us (9%)
  between operations  16 us (3%)
  starting transfers between devices  12.5 us (2%)
    psum x1, waiting for transfers between devices, shards(): gram_matrix = lax.psum(local_gram, ('grp', 'band')) / total_rows  121 us
    unnamed x3, waiting for transfers between devices  58.9 us
    all_to_all x1, waiting for transfers between devices, shards(): lax.all_to_all(spectra, 'band', split_axis=3, concat_axis=2, tiled=True)  49.1 us
    unnamed x8, local copies, waits for them, and re-layouts  45.3 us
    another operation x6, other arithmetic, shards(): lower_factor = jnp.linalg.cholesky(gram_matrix)  34 us
    reshape x2, local copies, waits for them, and re-layouts, shards(): spectra.astype(jnp.bfloat16)  29.7 us
    another operation x2, other arithmetic, shards(): jax.scipy.linalg.solve_triangular(lower_factor, jnp.eye(time_count, dtype...  19.9 us
    dot_general x1, matrix products, shards(): lax.dot_general(matrix, matrix, (((0,), (0,)), ((), ())), precision=lax.P...  17.8 us
  transfers between devices with their start and end apart: 3, of which 3 were waited for; matrix products, arithmetic and copies ran while one was open for 10% of the time, Pallas kernels for 0%

commit v1 on v0

v1 whole, which is shorter than its diff:
```python
import math

import jax
import jax.numpy as jnp
from jax import lax
from jax.experimental import pallas as pl
from jax.experimental.pallas import tpu as pltpu
from jax.sharding import PartitionSpec as P

F32 = jnp.float32
BF16 = jnp.bfloat16
AXES = ("grp", "band")


def cos_sin_quarter(position, lon_count):
    quarter = lon_count / 4.0
    turn = jnp.floor((position + quarter / 2.0) * (1.0 / quarter))
    angle = (position - turn * quarter) * (2.0 * math.pi / lon_count)
    square = angle * angle
    cosine = 1.0 + square * (-0.5 + square * (1.0 / 24 + square * (-1.0 / 720 + square * (1.0 / 40320))))
    sine = angle * (1.0 + square * (-1.0 / 6 + square * (1.0 / 120 + square * (-1.0 / 5040 + square * (1.0 / 362880)))))
    odd = (turn == 1.0) | (turn == 3.0)
    first = jnp.where(odd, sine, cosine)
    second = jnp.where(odd, cosine, sine)
    first = jnp.where((turn == 1.0) | (turn == 2.0), -first, first)
    second = jnp.where((turn == 2.0) | (turn == 3.0), -second, second)
    return first, second


def wrap(value, period):
    return value - period * jnp.floor((value + 0.5) * (1.0 / period))


def build_table(wave_ref, table_ref, lon_count):
    rows = table_ref.shape[0]
    step_rows = 32
    lanes = 128
    half_blocks = lon_count // lanes // 2

    def body(index, carry):
        at = pl.ds(pl.multiple_of(index * step_rows, step_rows), step_rows)
        wave = wave_ref[at, :]
        lane = lax.broadcasted_iota(jnp.int32, wave.shape, 1).astype(F32)
        row = lax.broadcasted_iota(jnp.int32, wave.shape, 0)
        quarter = jnp.where(row % 2 == 1, lon_count / 4.0, 0.0)
        real, imag = cos_sin_quarter(wrap(wave * lane + quarter, float(lon_count)), lon_count)
        turn_real, turn_imag = cos_sin_quarter(wrap(wave * float(lanes), float(lon_count)), lon_count)
        sign = 1.0 - 2.0 * wrap(wave, 2.0)
        for block in range(half_blocks):
            table_ref[at, block * lanes:(block + 1) * lanes] = real.astype(BF16)
            other = block + half_blocks
            table_ref[at, other * lanes:(other + 1) * lanes] = (real * sign).astype(BF16)
            if block + 1 < half_blocks:
                real, imag = real * turn_real - imag * turn_imag, real * turn_imag + imag * turn_real
        return carry

    lax.fori_loop(0, rows // step_rows, body, 0)


def fourier_kernel(wave_ref, field_ref, out_ref, table_ref):
    lon_count = field_ref.shape[3]

    @pl.when((pl.program_id(0) == 0) & (pl.program_id(1) == 0))
    def _():
        build_table(wave_ref, table_ref, lon_count)

    field = field_ref[0, 0]
    pairs = out_ref.shape[3]
    rows = table_ref.shape[0] // pairs
    for pair in range(pairs):
        result = lax.dot_general(
            table_ref[pair * rows:(pair + 1) * rows, :], field, (((1,), (1,)), ((), ())), preferred_element_type=F32
        )
        left = result[:, :128].reshape(rows // 8, 8, 128)
        right = result[:, 128:].reshape(rows // 8, 8, 128)
        low = lax.broadcasted_iota(jnp.int32, left.shape, 1) < 4
        even = jnp.where(low, left, pltpu.roll(right, 4, 1))
        odd = jnp.where(low, pltpu.roll(left, 4, 1), right)
        mixed = jnp.stack([even, odd], axis=1).reshape(rows // 4, 8, 128)
        out_ref[0, :, 0, pair] = mixed.astype(BF16)


def transform(fields, waves, bands):
    levels, lats, times, lon_count = fields.shape
    pairs = waves.shape[0] // (bands * 4)
    return pl.pallas_call(
        fourier_kernel,
        grid=(levels, lats),
        in_specs=[
            pl.BlockSpec(waves.shape, lambda l, i: (0, 0)),
            pl.BlockSpec((1, 1, times, lon_count), lambda l, i: (l, i, 0, 0)),
        ],
        out_specs=pl.BlockSpec((1, bands, 1, pairs, 8, 128), lambda l, i: (l, 0, i, 0, 0, 0)),
        out_shape=jax.ShapeDtypeStruct((levels, bands, lats, pairs, 8, 128), BF16),
        scratch_shapes=[pltpu.VMEM((waves.shape[0], lon_count), BF16)],
        name="fourier",
    )(waves, fields)


def legendre_kernel(spectra_ref, basis_ref, high_ref, low_ref, gram_ref, wide_ref, side_ref, cross_ref):
    step = pl.program_id(0)

    @pl.when(step == 0)
    def _():
        gram_ref[...] = jnp.zeros_like(gram_ref)
        cross_ref[...] = jnp.zeros_like(cross_ref)

    lats = spectra_ref.shape[0]
    wide_ref[...] = spectra_ref[:, 0].astype(F32).reshape(lats * 8, 128)
    for half in range(2):
        for h in range(2):
            for c in range(2):
                piece = wide_ref[pl.ds(half * 4 + h * 2 + c, lats, stride=8), :]
                side_ref[h, :, c * 256 + half * 128:c * 256 + half * 128 + 128] = piece.astype(BF16)
    product = jnp.dot(basis_ref[0, 0], side_ref[0], preferred_element_type=F32)
    product += jnp.dot(basis_ref[0, 1], side_ref[1], preferred_element_type=F32)
    flip = (((0,), (0,)), ((), ()))
    for c in range(2):
        value = product[:, c * 256:(c + 1) * 256]
        high = value.astype(BF16)
        low = (value - high.astype(F32)).astype(BF16)
        high_ref[0, c] = high
        low_ref[0, c] = low
        gram_ref[...] += lax.dot_general(high, high, flip, preferred_element_type=F32)
        gram_ref[...] += lax.dot_general(low, low, flip, preferred_element_type=F32)
        cross_ref[...] += lax.dot_general(high, low, flip, preferred_element_type=F32)

    @pl.when(step == pl.num_programs(0) - 1)
    def _():
        gram_ref[...] += cross_ref[...] + cross_ref[...].T


def project(spectra, legendre):
    lats, pairs = spectra.shape[:2]
    rows = legendre.shape[2]
    coefficient = jax.ShapeDtypeStruct((pairs, 2, rows, 256), BF16)
    block = pl.BlockSpec((1, 2, rows, 256), lambda q: (q, 0, 0, 0))
    return pl.pallas_call(
        legendre_kernel,
        grid=(pairs,),
        in_specs=[
            pl.BlockSpec((lats, 1, 8, 128), lambda q: (0, q, 0, 0)),
            pl.BlockSpec((1, 2, rows, lats), lambda q: (q, 0, 0, 0)),
        ],
        out_specs=[block, block, pl.BlockSpec((256, 256), lambda q: (0, 0))],
        out_shape=[coefficient, coefficient, jax.ShapeDtypeStruct((256, 256), F32)],
        scratch_shapes=[
            pltpu.VMEM((lats * 8, 128), F32),
            pltpu.VMEM((2, lats, 512), BF16),
            pltpu.VMEM((256, 256), F32),
        ],
        name="legendre",
    )(spectra, legendre)


def whiten_kernel(high_ref, low_ref, inverse_ref, out_ref):
    rows = out_ref.shape[2]
    inverse = inverse_ref[...]
    inverse_high = inverse.astype(BF16)
    inverse_low = (inverse - inverse_high.astype(F32)).astype(BF16)
    across = (((1,), (1,)), ((), ()))
    for c in range(2):
        value = lax.dot_general(high_ref[0, c], inverse_high, across, preferred_element_type=F32)
        value += lax.dot_general(high_ref[0, c], inverse_low, across, preferred_element_type=F32)
        value += lax.dot_general(low_ref[0, c], inverse_high, across, preferred_element_type=F32)
        out_ref[0, c] = value[:rows].astype(BF16)


def whiten(high, low, inverse, degree_rows):
    pairs, _, rows, _ = high.shape
    block = pl.BlockSpec((1, 2, rows, 256), lambda q: (q, 0, 0, 0))
    return pl.pallas_call(
        whiten_kernel,
        grid=(pairs,),
        in_specs=[block, block, pl.BlockSpec((256, 256), lambda q: (0, 0))],
        out_specs=pl.BlockSpec((1, 2, degree_rows, 256), lambda q: (q, 0, 0, 0)),
        out_shape=jax.ShapeDtypeStruct((pairs, 2, degree_rows, 256), BF16),
        name="whiten",
    )(high, low, inverse)


def exchange(value):
    return lax.all_to_all(value, AXES, split_axis=0, concat_axis=0, tiled=True)


def reduce_gram(gram, devices):
    pieces = gram.reshape(devices, -1, 128)
    total = exchange(pieces).sum(axis=0, keepdims=True)
    return exchange(jnp.broadcast_to(total, pieces.shape)).reshape(gram.shape)


def shards(fields, wave_order, basis):
    levels, times, lats, lon_count = fields.shape
    groups, bands = lax.axis_size("grp"), lax.axis_size("band")
    pairs, _, lat_total, degree_rows = basis.shape
    padded_rows = -(-degree_rows // 16) * 16
    waves = wave_order.reshape(bands, pairs, 2).transpose(1, 0, 2).reshape(-1)
    waves = jnp.broadcast_to(jnp.repeat(waves, 2)[:, None], (waves.shape[0] * 2, 128)).astype(F32)
    sent = transform(fields.transpose(0, 2, 1, 3), waves, bands)
    received = exchange(sent.reshape(groups * bands, lats, pairs, 8, 128))
    legendre = jnp.pad(basis.transpose(0, 1, 3, 2), ((0, 0), (0, 0), (0, padded_rows - degree_rows), (0, 0)))
    high, low, local_gram = project(received.reshape(lat_total, pairs, 8, 128), legendre)
    total_rows = levels * pairs * bands * 2 * degree_rows
    gram_matrix = reduce_gram(local_gram, groups * bands) / total_rows
    lower_factor = jnp.linalg.cholesky(gram_matrix)
    inverse = jax.scipy.linalg.solve_triangular(lower_factor, jnp.eye(times, dtype=F32), lower=True)
    whitened = whiten(high, low, inverse, degree_rows)
    return (whitened[None], lower_factor.T)


def solution(mesh):
    placed = (P(None, None, ("grp", "band"), None), P(), P("band", None, None, None))
    return jax.shard_map(
        shards,
        mesh=mesh,
        in_specs=placed,
        out_specs=(P("grp", "band", None, None, None), P()),
        check_vma=False,
    )
```

time: 561 us -> 250 us (0.45); the launches traced: 550 us -> 248 us
  waiting for transfers between devices: 229 us -> 82.7 us
  local copies, waits for them, and re-layouts: 173 us -> 29.8 us
  matrix products: 48.9 us -> 1.31 us
  Pallas kernels: 0 us -> 39.3 us
  blocking collectives: 0 us -> 21.1 us
  other arithmetic: 70.9 us -> 55.7 us
  between operations: 16 us -> 2.16 us
    psum x1 -> x0, waiting for transfers between devices: 121 us -> none  [shards(): gram_matrix = lax.psum(local_gram, ('grp', 'band')) / total_rows]
    unnamed x3 -> x0, waiting for transfers between devices: 58.9 us -> none
    reshape x5 -> x1, local copies, waits for them, and re-layouts: 53.6 us -> 1.07 us  [reduce_gram(): pieces = gram.reshape(devices, -1, 128)]
    dot_general x4 -> x0, matrix products: 47.6 us -> none  [the longest x1 17.8 us: shards(): lax.dot_general(matrix, matrix, (((0,), (0,)), ((), ())), precision=lax.P...]
    pallas_call x0 -> x3, Pallas kernels: none -> 39.3 us  [the longest x1 17 us: transform(): pl.pallas_call(fourier_kernel, grid=(levels, lats), in_specs=[pl.BlockSpe...]
    all_to_all x1 -> x2, waiting for transfers between devices: 49.1 us -> 82.7 us  [exchange(): return lax.all_to_all(value, AXES, split_axis=0, concat_axis=0, tiled=True)]
    unnamed x8 -> x3, local copies, waits for them, and re-layouts: 45.3 us -> 14.6 us
    all_to_all x0 -> x1, blocking collectives: none -> 21.1 us  [exchange(): return lax.all_to_all(value, AXES, split_axis=0, concat_axis=0, tiled=True)]
  transfers between devices with their start and end apart: 3 -> 2, of which waited for: 3 -> 2; matrix products, arithmetic and copies ran while one was open for 10% -> 6% of each run, Pallas kernels for 0% -> 0%
where the time goes in v1:
time: 250 us; the launch traced here: 248 us
  waiting for transfers between devices  82.7 us (33%)
  other arithmetic  55.7 us (22%)
  Pallas kernels  39.3 us (16%)
  local copies, waits for them, and re-layouts  29.8 us (12%)
  blocking collectives  21.1 us (8%)
  starting transfers between devices  16.4 us (7%)
    all_to_all x2, waiting for transfers between devices, exchange(): return lax.all_to_all(value, AXES, split_axis=0, concat_axis=0, tiled=True)  82.7 us
    another operation x6, other arithmetic, shards(): lower_factor = jnp.linalg.cholesky(gram_matrix)  34 us
    all_to_all x1, blocking collectives, exchange(): return lax.all_to_all(value, AXES, split_axis=0, concat_axis=0, tiled=True)  21.1 us
    another operation x3, other arithmetic, shards(): jax.scipy.linalg.solve_triangular(lower_factor, jnp.eye(times, dtype=F32)...  20.6 us
    pallas_call x1, Pallas kernels, transform(): pl.pallas_call(fourier_kernel, grid=(levels, lats), in_specs=[pl.BlockSpe...  17 us
    all_to_all x2, starting transfers between devices, exchange(): return lax.all_to_all(value, AXES, split_axis=0, concat_axis=0, tiled=True)  16.4 us
    pallas_call x1, Pallas kernels, project(): pl.pallas_call(legendre_kernel, grid=(pairs,), in_specs=[pl.BlockSpec((la...  14.8 us
    unnamed x3, local copies, waits for them, and re-layouts  14.6 us
  transfers between devices with their start and end apart: 2, of which 2 were waited for; matrix products, arithmetic and copies ran while one was open for 6% of the time, Pallas kernels for 0%

profile of v1, /device:TPU:1, one launch (start us, length us, event | category | flops | bytes accessed | tf_op | source)
XLA Modules:
  0.0 248.5 jit_solution(6668381189020633947)
XLA Ops:
  0.6 0.7 convert_element_type.14
  1.3 0.1 convert_element_type.15
  1.5 0.1 convert_element_type.17
  1.6 0.1 broadcast_in_dim.10
  1.8 0.2 convert_element_type.18
  2.0 1.1 broadcast_in_dim.20.wave_ref
  3.1 17.0 %fourier.1 = bf16[2,64,5,5,8,128]{5,4,3,2,1,0:T(8,128)(2,1)} custom-call(f32[1280,128]{1,0:T(8,128)} %broadcast_in_dim.20.wave_ref, bf16[2,5,256,1280]{3,2,1,0:T(8,128)(2,1)} %bitcast.44), custom_call_target="tpu_custom_call" | custom-call | tf_op jit(solution)/shard_map/fourier/pallas_call | solution.py:86
  20.1 11.9 %all-to-all-start = ((bf16[128,5,5,8,128]{4,3,2,1,0:T(8,128)(2,1)}), bf16[128,5,5,8,128]{4,3,2,1,0:T(8,128)(2,1)}, u32[]{:S(2)}, u32[]{:S(2)}) async-start(bf16[128,5,5,8,128]{4,3,2,1,0:T(8,128)(2,1)} %bitcast.42), calls=%async_computation | async-start | bytes 13107200 | tf_op jit(solution)/shard_map/all_to_all | solution.py:183
  32.0 7.6 %copy.15 = bf16[5,2,640,641]{2,3,1,0:T(8,128)(2,1)} copy(bf16[5,2,640,641]{2,1,3,0:T(2,128)(2,1)} %param.5) | data formatting | bytes 16409600 | tf_op args[2]
  39.6 7.3 %pad.5.basis_ref = bf16[5,2,656,640]{3,2,1,0:T(8,128)(2,1)} pad(bf16[5,2,641,640]{3,2,1,0:T(8,128)(2,1)} %bitcast.41, bf16[]{:T(256)} %constant.79.clone.1), padding=0_0x0_0x0_15x0_0 | pad | bytes 16601602 | tf_op jit(solution)/shard_map/jit(_pad)/pad | solution.py:201
  46.9 72.1 %all-to-all-done = bf16[128,5,5,8,128]{4,3,2,1,0:T(8,128)(2,1)} async-done(((bf16[128,5,5,8,128]{4,3,2,1,0:T(8,128)(2,1)}), bf16[128,5,5,8,128]{4,3,2,1,0:T(8,128)(2,1)}, u32[]{:S(2)}, u32[]{:S(2)}) %all-to-all-start) | async-done | bytes 6553632 | tf_op jit(solution)/shard_map/all_to_all | solution.py:183
  119.0 14.8 %legendre.1 = (bf16[5,2,656,256]{3,2,1,0:T(8,128)(2,1)}, bf16[5,2,656,256]{3,2,1,0:T(8,128)(2,1)}, f32[256,256]{1,0:T(8,128)}) custom-call(bf16[640,5,8,128]{3,2,1,0:T(8,128)(2,1)} %bitcast.3.spectra_ref, bf16[5,2,656,640]{3,2,1,0:T(8,128)(2,1)} %pad.5.basis_ref), custom_call_target="tpu_custom_call" | custom-call | tf_op jit(solution)/shard_map/legendre/pallas_call | solution.py:138
  133.7 1.1 reshape.44
  134.8 21.1 %all_to_all.15 = f32[128,4,128]{2,1,0:T(4,128)S(1)} all-to-all(f32[128,4,128]{2,1,0:T(4,128)S(1)} %reshape.44), channel_id=1, replica_groups=mesh['grp'=2,'band'=64] {'grp','band'}, dimensions={0} | all-to-all | bytes 524288 | tf_op jit(solution)/shard_map/all_to_all | solution.py:183
  156.0 0.1 reduce_sum.9
  156.1 0.7 broadcast_in_dim.21
  156.8 4.5 %all-to-all-start.2 = ((f32[128,4,128]{2,1,0:T(4,128)}), f32[128,4,128]{2,1,0:T(4,128)S(1)}, u32[]{:S(2)}, u32[]{:S(2)}) async-start(f32[128,4,128]{2,1,0:T(4,128)} %broadcast_in_dim.21), calls=%async_computation.2 | async-start | bytes 524288 | tf_op jit(solution)/shard_map/all_to_all | solution.py:183
  161.4 10.5 %all-to-all-done.2 = f32[128,4,128]{2,1,0:T(4,128)S(1)} async-done(((f32[128,4,128]{2,1,0:T(4,128)}), f32[128,4,128]{2,1,0:T(4,128)S(1)}, u32[]{:S(2)}, u32[]{:S(2)}) %all-to-all-start.2) | async-done | bytes 262176 | tf_op jit(solution)/shard_map/all_to_all | solution.py:183
  172.0 0.1 broadcast_multiply_fusion
  172.1 0.1 div.18
  172.2 0.1 copy.11
  172.4 11.7 %cholesky.50 = f32[128,128]{1,0:T(8,128)S(1)} custom-call(f32[128,128]{1,0:T(8,128)S(1)} %cholesky.118), custom_call_target="Cholesky" | custom-call | tf_op jit(solution)/shard_map/jit(cholesky)/cholesky | solution.py:205
  184.2 9.8 %custom-call.15 = f32[1,128,128]{1,2,0:T(8,128)S(1)} custom-call(f32[1,128,128]{2,1,0:T(8,128)S(1)} %get-tuple-element.35), custom_call_target="InvertDiagBlocksLowerTriangular" | custom-call | tf_op jit(solution)/shard_map/jit(cholesky)/cholesky | solution.py:205
  194.0 0.2 constant_dynamic-update-slice_fusion.1
  194.2 0.3 convolution_subtract_fusion.1
  194.5 11.7 %cholesky.105 = f32[128,128]{1,0:T(8,128)S(1)} custom-call(f32[128,128]{1,0:T(8,128)S(1)} %convolution_subtract_fusion.1), custom_call_target="Cholesky" | custom-call | tf_op jit(solution)/shard_map/jit(cholesky)/cholesky | solution.py:205
  206.2 0.7 compare_reduce_fusion
  208.3 0.1 triangular_solve.63
  208.4 4.1 %while.1 = (s32[]{:T(128)}, f32[256,256]{1,0:T(8,128)S(1)}, s32[2,2]{1,0:T(2,128)S(1)}, f32[2,128,128]{2,1,0:T(8,128)S(1)}, s32[]{:T(128)}) while((s32[]{:T(128)}, f32[256,256]{1,0:T(8,128)S(1)}, s32[2,2]{1,0:T(2,128)S(1)}, f32[2,128,128]{2,1,0:T(8,128)S(1)}, s32[]{:T(128)}) %tuple.30), condition=%wide.while_cond, body=%wide.while_body.sunk | while | flops 2 | bytes 131181 | solution.py:206
  208.4 0.6 fusion.16
  209.0 1.4 bitcast_dynamic-update-slice_fusion.2
  210.5 0.6 fusion.16
  211.1 1.4 bitcast_dynamic-update-slice_fusion.2
  212.5 19.9 %custom-call.16 = f32[2,128,128]{1,2,0:T(8,128)S(1)} custom-call(f32[2,128,128]{2,1,0:T(8,128)S(1)} %get-tuple-element.15), custom_call_target="InvertDiagBlocksLowerTriangular" | custom-call | tf_op jit(solution)/shard_map/jit(_solve_triangular)/triangular_solve | solution.py:206
  232.4 0.3 fusion.3
  232.7 0.3 convolution_subtract_fusion
  232.9 0.3 fusion.6
  233.3 0.7 pad_maximum_fusion.inverse_ref
  234.0 7.5 %whiten.1 = bf16[5,2,641,256]{3,2,1,0:T(8,128)(2,1)} custom-call(bf16[5,2,656,256]{3,2,1,0:T(8,128)(2,1)} %get-tuple-element.5.high_ref, bf16[5,2,656,256]{3,2,1,0:T(8,128)(2,1)} %get-tuple-element.6.low_ref, f32[256,256]{1,0:T(8,128)} %pad_maximum_fusion.inverse_ref), custom_call_target="tpu_custom_call" | custom-call | tf_op jit(solution)/shard_map/whiten/pallas_call | solution.py:172
  241.5 6.2 %copy.12 = bf16[1,5,2,641,256]{4,2,3,1,0:T(2,128)(2,1)} copy(bf16[1,5,2,641,256]{4,3,2,1,0:T(8,128)(2,1)} %bitcast.43) | data formatting | bytes 6563840
  247.7 0.8 copy.13
  (12 shorter events, 0.3 us)
Async XLA Ops:
  20.1 98.9 %all-to-all-start = ((bf16[128,5,5,8,128]{4,3,2,1,0:T(8,128)(2,1)}), bf16[128,5,5,8,128]{4,3,2,1,0:T(8,128)(2,1)}, u32[]{:S(2)}, u32[]{:S(2)}) async-start(bf16[128,5,5,8,128]{4,3,2,1,0:T(8,128)(2,1)} %bitcast.42), calls=%async_computation | async-start | bytes 13107200 | tf_op jit(solution)/shard_map/all_to_all | solution.py:183
  156.8 15.1 %all-to-all-start.2 = ((f32[128,4,128]{2,1,0:T(4,128)}), f32[128,4,128]{2,1,0:T(4,128)S(1)}, u32[]{:S(2)}, u32[]{:S(2)}) async-start(f32[128,4,128]{2,1,0:T(4,128)} %broadcast_in_dim.21), calls=%async_computation.2 | async-start | bytes 524288 | tf_op jit(solution)/shard_map/all_to_all | solution.py:183

commit v2 on v1

v2 whole, which is shorter than its diff:
```python
import functools
import math

import jax
import jax.numpy as jnp
from jax import lax
from jax.experimental import pallas as pl
from jax.experimental.pallas import tpu as pltpu
from jax.sharding import PartitionSpec as P

F32 = jnp.float32
BF16 = jnp.bfloat16
AXES = ("grp", "band")
CHUNKS = (2, 3)


def cos_sin_quarter(position, lon_count):
    quarter = lon_count / 4.0
    turn = jnp.floor((position + quarter / 2.0) * (1.0 / quarter))
    angle = (position - turn * quarter) * (2.0 * math.pi / lon_count)
    square = angle * angle
    cosine = 1.0 + square * (-0.5 + square * (1.0 / 24 + square * (-1.0 / 720 + square * (1.0 / 40320))))
    sine = angle * (1.0 + square * (-1.0 / 6 + square * (1.0 / 120 + square * (-1.0 / 5040 + square * (1.0 / 362880)))))
    odd = (turn == 1.0) | (turn == 3.0)
    first = jnp.where(odd, sine, cosine)
    second = jnp.where(odd, cosine, sine)
    first = jnp.where((turn == 1.0) | (turn == 2.0), -first, first)
    second = jnp.where((turn == 2.0) | (turn == 3.0), -second, second)
    return first, second


def wrap(value, period):
    return value - period * jnp.floor((value + 0.5) * (1.0 / period))


def build_table(chunk, pairs_total, orders_ref, wave_ref, table_ref, lon_count):
    start, pairs = chunk
    lanes = 128
    step_rows = 32
    half_blocks = lon_count // lanes // 2
    rows = table_ref.shape[0] // pairs
    orders = orders_ref[...].astype(F32)
    high = jnp.floor((orders + 0.5) * (1.0 / 32))
    low = orders - 32.0 * high
    high = jnp.broadcast_to(high, (lanes, high.shape[1])).astype(BF16)
    low = jnp.broadcast_to(low, (lanes, low.shape[1])).astype(BF16)
    shape = (rows, orders.shape[1])
    row = lax.broadcasted_iota(jnp.int32, shape, 0)
    slot = lax.broadcasted_iota(jnp.int32, shape, 1)
    across = (((1,), (1,)), ((), ()))
    for pair in range(pairs):
        wanted = (row // 4) * (2 * pairs_total) + 2 * (start + pair) + (row // 2) % 2
        choice = jnp.where(slot == wanted, 1.0, 0.0).astype(BF16)
        wave_ref[pair * rows:(pair + 1) * rows, :] = 32.0 * lax.dot_general(
            choice, high, across, preferred_element_type=F32
        ) + lax.dot_general(choice, low, across, preferred_element_type=F32)

    def body(index, carry):
        at = pl.ds(pl.multiple_of(index * step_rows, step_rows), step_rows)
        wave = wave_ref[at, :]
        lane = lax.broadcasted_iota(jnp.int32, wave.shape, 1).astype(F32)
        parity = lax.broadcasted_iota(jnp.int32, wave.shape, 0) % 2
        quarter = jnp.where(parity == 1, lon_count / 4.0, 0.0)
        real, imag = cos_sin_quarter(wrap(wave * lane + quarter, float(lon_count)), lon_count)
        turn_real, turn_imag = cos_sin_quarter(wrap(wave * float(lanes), float(lon_count)), lon_count)
        sign = 1.0 - 2.0 * wrap(wave, 2.0)
        for block in range(half_blocks):
            table_ref[at, block * lanes:(block + 1) * lanes] = real.astype(BF16)
            other = block + half_blocks
            table_ref[at, other * lanes:(other + 1) * lanes] = (real * sign).astype(BF16)
            if block + 1 < half_blocks:
                real, imag = real * turn_real - imag * turn_imag, real * turn_imag + imag * turn_real
        return carry

    lax.fori_loop(0, table_ref.shape[0] // step_rows, body, 0)


def fourier_kernel(chunk, pairs_total, orders_ref, field_ref, out_ref, wave_ref, table_ref):
    lon_count = field_ref.shape[3]

    @pl.when((pl.program_id(0) == 0) & (pl.program_id(1) == 0))
    def _():
        build_table(chunk, pairs_total, orders_ref, wave_ref, table_ref, lon_count)

    field = field_ref[0, 0]
    pairs = chunk[1]
    rows = table_ref.shape[0] // pairs
    for pair in range(pairs):
        result = lax.dot_general(
            table_ref[pair * rows:(pair + 1) * rows, :], field, (((1,), (1,)), ((), ())), preferred_element_type=F32
        )
        left = result[:, :128].reshape(rows // 8, 8, 128)
        right = result[:, 128:].reshape(rows // 8, 8, 128)
        low = lax.broadcasted_iota(jnp.int32, left.shape, 1) < 4
        even = jnp.where(low, left, pltpu.roll(right, 4, 1))
        odd = jnp.where(low, pltpu.roll(left, 4, 1), right)
        mixed = jnp.stack([even, odd], axis=1).reshape(rows // 4, 8, 128)
        out_ref[0, :, 0, pair] = mixed.astype(BF16)


def transform(fields, orders, bands, pairs_total, chunk):
    levels, lats, times, lon_count = fields.shape
    pairs = chunk[1]
    rows = pairs * bands * 4
    return pl.pallas_call(
        functools.partial(fourier_kernel, chunk, pairs_total),
        grid=(levels, lats),
        in_specs=[
            pl.BlockSpec(orders.shape, lambda l, i: (0, 0)),
            pl.BlockSpec((1, 1, times, lon_count), lambda l, i: (l, i, 0, 0)),
        ],
        out_specs=pl.BlockSpec((1, bands, 1, pairs, 8, 128), lambda l, i: (l, 0, i, 0, 0, 0)),
        out_shape=jax.ShapeDtypeStruct((levels, bands, lats, pairs, 8, 128), BF16),
        scratch_shapes=[pltpu.VMEM((rows, 128), F32), pltpu.VMEM((rows, lon_count), BF16)],
        cost_estimate=pl.CostEstimate(
            flops=2 * rows * levels * lats * times * lon_count,
            bytes_accessed=2 * levels * lats * times * (lon_count + rows),
            transcendentals=0,
        ),
        name="fourier",
    )(orders, fields)


def legendre_kernel(later, spectra_ref, basis_ref, *refs):
    if later:
        before_ref, refs = refs[2], refs[3:]
    high_ref, low_ref, gram_ref, wide_ref, side_ref, cross_ref = refs
    step = pl.program_id(0)

    @pl.when(step == 0)
    def _():
        gram_ref[...] = before_ref[...] if later else jnp.zeros_like(gram_ref)
        cross_ref[...] = jnp.zeros_like(cross_ref)

    lats = spectra_ref.shape[0]
    wide_ref[...] = spectra_ref[:, 0].astype(F32).reshape(lats * 8, 128)
    for half in range(2):
        for h in range(2):
            for c in range(2):
                piece = wide_ref[pl.ds(half * 4 + h * 2 + c, lats, stride=8), :]
                side_ref[h, :, c * 256 + half * 128:c * 256 + half * 128 + 128] = piece.astype(BF16)
    product = jnp.dot(basis_ref[0, 0], side_ref[0], preferred_element_type=F32)
    product += jnp.dot(basis_ref[0, 1], side_ref[1], preferred_element_type=F32)
    flip = (((0,), (0,)), ((), ()))
    for c in range(2):
        value = product[:, c * 256:(c + 1) * 256]
        high = value.astype(BF16)
        low = (value - high.astype(F32)).astype(BF16)
        high_ref[0, c] = high
        low_ref[0, c] = low
        gram_ref[...] += lax.dot_general(high, high, flip, preferred_element_type=F32)
        gram_ref[...] += lax.dot_general(low, low, flip, preferred_element_type=F32)
        cross_ref[...] += lax.dot_general(high, low, flip, preferred_element_type=F32)

    @pl.when(step == pl.num_programs(0) - 1)
    def _():
        gram_ref[...] += cross_ref[...] + cross_ref[...].T


def project(spectra, legendre, start, carried):
    lats, pairs = spectra.shape[:2]
    pairs_total, _, rows, _ = legendre.shape
    coefficient = jax.ShapeDtypeStruct((pairs_total, 2, rows, 256), BF16)
    block = pl.BlockSpec((1, 2, rows, 256), lambda q: (q + start, 0, 0, 0))
    whole = pl.BlockSpec((256, 256), lambda q: (0, 0))
    later = carried is not None
    kept = pl.BlockSpec(memory_space=pl.ANY)
    return pl.pallas_call(
        functools.partial(legendre_kernel, later),
        grid=(pairs,),
        in_specs=[
            pl.BlockSpec((lats, 1, 8, 128), lambda q: (0, q, 0, 0)),
            pl.BlockSpec((1, 2, rows, lats), lambda q: (q + start, 0, 0, 0)),
        ] + ([kept, kept, whole] if later else []),
        out_specs=[block, block, whole],
        out_shape=[coefficient, coefficient, jax.ShapeDtypeStruct((256, 256), F32)],
        scratch_shapes=[
            pltpu.VMEM((lats * 8, 128), F32),
            pltpu.VMEM((2, lats, 512), BF16),
            pltpu.VMEM((256, 256), F32),
        ],
        input_output_aliases={2: 0, 3: 1} if later else {},
        cost_estimate=pl.CostEstimate(
            flops=pairs * (4 * rows * lats * 512 + 12 * rows * 256 * 256),
            bytes_accessed=pairs * (lats * 2048 + 4 * rows * lats + rows * 2048),
            transcendentals=0,
        ),
        name="legendre",
    )(spectra, legendre, *(carried or ()))


def factor_block(groups):
    count = len(groups)
    n = count * 8
    shape = (8, n)
    lane = lax.broadcasted_iota(jnp.int32, shape, 1)
    sub = lax.broadcasted_iota(jnp.int32, shape, 0)
    work = list(groups)
    upper, inverse = [jnp.zeros(shape, F32)] * count, [jnp.zeros(shape, F32)] * count
    for j in range(0, n, 2):
        g, r = divmod(j, 8)
        col0 = [jnp.broadcast_to(work[k][:, j:j + 1], shape) for k in range(g, count)]
        col1 = [jnp.broadcast_to(work[k][:, j + 1:j + 2], shape) for k in range(g, count)]
        p = jnp.broadcast_to(col0[0][r:r + 1], shape)
        q = jnp.broadcast_to(col0[0][r + 1:r + 2], shape)
        s = jnp.broadcast_to(col1[0][r + 1:r + 2], shape)
        row0 = jnp.broadcast_to(work[g][r:r + 1], shape)
        row1 = jnp.broadcast_to(work[g][r + 1:r + 2], shape)
        over0 = 1.0 / p
        ratio = q * over0
        rest = s - q * ratio
        over1 = 1.0 / rest
        first, second = lane == j, lane == j + 1
        unit0 = jnp.where(first, 1.0, jnp.where(second, 0.0, row0))
        unit1 = jnp.where(second, 1.0, jnp.where(first, 0.0, row1)) - ratio * unit0
        down0, down1 = unit0 * over0, unit1 * over1
        pair = first | second
        for k in range(g, count):
            moved = jnp.where(pair, 0.0, work[k]) - col0[k - g] * down0 - (col1[k - g] - ratio * col0[k - g]) * down1
            work[k] = moved if k > g else jnp.where(sub > r + 1, moved, work[k])
        root0, root1 = lax.rsqrt(p), lax.rsqrt(rest)
        up0 = jnp.where(lane >= j, row0, 0.0) * root0
        up1 = jnp.where(lane >= j + 1, row1 - ratio * row0, 0.0) * root1
        inv0 = jnp.where(lane <= j, unit0, 0.0) * root0
        inv1 = jnp.where(lane <= j + 1, unit1, 0.0) * root1
        upper[g] = jnp.where(sub == r, up0, jnp.where(sub == r + 1, up1, upper[g]))
        inverse[g] = jnp.where(sub == r, inv0, jnp.where(sub == r + 1, inv1, inverse[g]))
    return jnp.concatenate(upper, 0), jnp.concatenate(inverse, 0)


def f32_dot(a, b, dims=(((1,), (0,)), ((), ()))):
    return lax.dot_general(a, b, dims, precision=lax.Precision.HIGHEST, preferred_element_type=F32)


def factor_into(scale, gram_ref, factor_ref, inverse_ref, block_ref):
    half = gram_ref.shape[0] // 2
    flip = (((0,), (0,)), ((), ()))
    block_ref[...] = gram_ref[:half, :half] * scale

    def step(index, carry):
        upper, inverse = factor_block([block_ref[k * 8:(k + 1) * 8, :] for k in range(half // 8)])

        @pl.when(index == 0)
        def _():
            factor_ref[:half, :half] = upper
            inverse_ref[:half, :half] = inverse
            side = f32_dot(inverse, gram_ref[:half, half:] * scale)
            factor_ref[:half, half:] = side
            block_ref[...] = gram_ref[half:, half:] * scale - f32_dot(side, side, flip)

        @pl.when(index == 1)
        def _():
            factor_ref[half:, half:] = upper
            inverse_ref[half:, half:] = inverse
            below = f32_dot(factor_ref[:half, half:], inverse_ref[:half, :half], flip)
            inverse_ref[half:, :half] = -f32_dot(inverse, below)

        return carry

    lax.fori_loop(0, 2, step, 0)
    factor_ref[half:, :half] = jnp.zeros((half, half), F32)
    inverse_ref[:half, half:] = jnp.zeros((half, half), F32)


def finish_kernel(scale, gram_ref, high_ref, low_ref, out_ref, factor_ref, inverse_ref, block_ref, top_ref, rest_ref):
    @pl.when(pl.program_id(0) == 0)
    def _():
        factor_into(scale, gram_ref, factor_ref, inverse_ref, block_ref)
        inverse = inverse_ref[...]
        top = inverse.astype(BF16)
        top_ref[...] = top
        rest_ref[...] = (inverse - top.astype(F32)).astype(BF16)

    rows = out_ref.shape[1]
    across = (((1,), (1,)), ((), ()))
    for c in range(2):
        value = lax.dot_general(high_ref[0, c], top_ref[...], across, preferred_element_type=F32)
        value += lax.dot_general(high_ref[0, c], rest_ref[...], across, preferred_element_type=F32)
        value += lax.dot_general(low_ref[0, c], top_ref[...], across, preferred_element_type=F32)
        out_ref[0, :, c, :] = value[:rows].astype(BF16)


def finish(gram, high, low, total_rows, degree_rows):
    pairs, _, rows, _ = high.shape
    block = pl.BlockSpec((1, 2, rows, 256), lambda q: (q, 0, 0, 0))
    whole = pl.BlockSpec((256, 256), lambda q: (0, 0))
    return pl.pallas_call(
        functools.partial(finish_kernel, 1.0 / total_rows),
        grid=(pairs,),
        in_specs=[whole, block, block],
        out_specs=[pl.BlockSpec((1, degree_rows, 2, 256), lambda q: (q, 0, 0, 0)), whole],
        out_shape=[
            jax.ShapeDtypeStruct((pairs, degree_rows, 2, 256), BF16),
            jax.ShapeDtypeStruct((256, 256), F32),
        ],
        scratch_shapes=[
            pltpu.VMEM((256, 256), F32),
            pltpu.VMEM((128, 128), F32),
            pltpu.VMEM((256, 256), BF16),
            pltpu.VMEM((256, 256), BF16),
        ],
        name="finish",
    )(gram, high, low)


def exchange(value):
    return lax.all_to_all(value, AXES, split_axis=0, concat_axis=0, tiled=True)


def reduce_gram(gram, devices):
    pieces = gram.reshape(devices, -1, 128)
    total = exchange(pieces).sum(axis=0, keepdims=True)
    return exchange(jnp.broadcast_to(total, pieces.shape)).reshape(gram.shape)


def shards(fields, wave_order, basis):
    levels, times, lats, lon_count = fields.shape
    groups, bands = lax.axis_size("grp"), lax.axis_size("band")
    pairs, _, lat_total, degree_rows = basis.shape
    padded_rows = -(-degree_rows // 16) * 16
    fields = fields.transpose(0, 2, 1, 3)
    orders = wave_order.reshape(1, -1)
    starts = [sum(CHUNKS[:n]) for n in range(len(CHUNKS))]
    received = []
    for chunk in zip(starts, CHUNKS):
        sent = transform(fields, orders, bands, pairs, chunk)
        received.append(exchange(sent.reshape(groups * bands, lats, chunk[1], 8, 128)))
    legendre = jnp.pad(basis.transpose(0, 1, 3, 2), ((0, 0), (0, 0), (0, padded_rows - degree_rows), (0, 0)))
    carried = None
    for start, spectra in zip(starts, received):
        carried = project(spectra.reshape(lat_total, -1, 8, 128), legendre, start, carried)
    high, low, local_gram = carried
    gram = reduce_gram(local_gram, groups * bands)
    whitened, factor = finish(gram, high, low, levels * pairs * bands * 2 * degree_rows, degree_rows)
    return (whitened.transpose(0, 2, 1, 3)[None], factor)


def solution(mesh):
    placed = (P(None, None, ("grp", "band"), None), P(), P("band", None, None, None))
    return jax.shard_map(
        shards,
        mesh=mesh,
        in_specs=placed,
        out_specs=(P("grp", "band", None, None, None), P()),
        check_vma=False,
    )
```

time: 250 us -> 199 us (0.80)
  other arithmetic: 55.7 us -> 0.14 us
  waiting for transfers between devices: 82.7 us -> 45.7 us
  Pallas kernels: 39.3 us -> 73.2 us
  blocking collectives: 21.1 us -> 39.4 us
  local copies, waits for them, and re-layouts: 29.8 us -> 19.6 us
  starting transfers between devices: 16.4 us -> 19.4 us
    another operation x9 -> x0, other arithmetic: 54.6 us -> none  [the longest x6 34 us: shards(): lower_factor = jnp.linalg.cholesky(gram_matrix)]
    all_to_all x2, waiting for transfers between devices: 82.7 us -> 45.7 us  [exchange(): return lax.all_to_all(value, AXES, split_axis=0, concat_axis=0, tiled=True)]
    pallas_call x3 -> x5, Pallas kernels: 39.3 us -> 73.2 us  [the longest x1 29.7 us: finish(): pl.pallas_call(functools.partial(finish_kernel, 1.0 / total_rows), grid=(...]
    all_to_all x1 -> x2, blocking collectives: 21.1 us -> 39.4 us  [exchange(): return lax.all_to_all(value, AXES, split_axis=0, concat_axis=0, tiled=True)]
    unnamed x3, local copies, waits for them, and re-layouts: 14.6 us -> 9.07 us
    another operation x9 -> x0, local copies, waits for them, and re-layouts: 4.16 us -> none
    all_to_all x2, starting transfers between devices: 16.4 us -> 19.4 us  [exchange(): return lax.all_to_all(value, AXES, split_axis=0, concat_axis=0, tiled=True)]
  transfers between devices with their start and end apart: 2 -> 2, of which waited for: 2 -> 2; matrix products, arithmetic and copies ran while one was open for 6% -> 8% of each run, Pallas kernels for 0% -> 11%
where the time goes in v2:
time: 199 us; the launch traced here: 198 us
  Pallas kernels  73.2 us (37%)
  waiting for transfers between devices  45.7 us (23%)
  blocking collectives  39.4 us (20%)
  local copies, waits for them, and re-layouts  19.6 us (10%)
  starting transfers between devices  19.4 us (10%)
    all_to_all x2, waiting for transfers between devices, exchange(): return lax.all_to_all(value, AXES, split_axis=0, concat_axis=0, tiled=True)  45.7 us
    all_to_all x2, blocking collectives, exchange(): return lax.all_to_all(value, AXES, split_axis=0, concat_axis=0, tiled=True)  39.4 us
    pallas_call x1, Pallas kernels, finish(): pl.pallas_call(functools.partial(finish_kernel, 1.0 / total_rows), grid=(...  29.7 us
    pallas_call x2, Pallas kernels, transform(): pl.pallas_call(functools.partial(fourier_kernel, chunk, pairs_total), gri...  25.6 us
    all_to_all x2, starting transfers between devices, exchange(): return lax.all_to_all(value, AXES, split_axis=0, concat_axis=0, tiled=True)  19.4 us
    pallas_call x2, Pallas kernels, project(): pl.pallas_call(functools.partial(legendre_kernel, later), grid=(pairs,),...  17.9 us
    unnamed x3, local copies, waits for them, and re-layouts  9.07 us
    pad x1, local copies, waits for them, and re-layouts, shards(): jnp.pad(basis.transpose(0, 1, 3, 2), ((0, 0), (0, 0), (0, padded_rows - d...  7.3 us
  transfers between devices with their start and end apart: 2, of which 2 were waited for; matrix products, arithmetic and copies ran while one was open for 8% of the time, Pallas kernels for 11%

profile of v2, /device:TPU:1, one launch (start us, length us, event | category | flops | bytes accessed | tf_op | source)
XLA Modules:
  0.0 198.1 jit_solution(2890471228397354361)
XLA Ops:
  0.6 1.3 reshape.26.orders_ref
  1.9 11.8 %fourier.3 = bf16[2,64,5,2,8,128]{5,4,3,2,1,0:T(8,128)(2,1)} custom-call(s32[1,640]{1,0:T(1,128)} %reshape.26.orders_ref, bf16[2,5,256,1280]{3,2,1,0:T(8,128)(2,1)} %bitcast.15), custom_call_target="tpu_custom_call" | custom-call | flops 3355443200 | bytes 9175040 | tf_op jit(solution)/shard_map/fourier/pallas_call | solution.py:105
  13.7 11.5 %all-to-all-start.1 = ((bf16[128,5,2,8,128]{4,3,2,1,0:T(8,128)(2,1)}), bf16[128,5,2,8,128]{4,3,2,1,0:T(8,128)(2,1)S(1)}, u32[]{:S(2)}, u32[]{:S(2)}) async-start(bf16[128,5,2,8,128]{4,3,2,1,0:T(8,128)(2,1)} %bitcast.14), calls=%async_computation.1 | async-start | bytes 5242880 | tf_op jit(solution)/shard_map/all_to_all | solution.py:307
  25.2 13.9 %fourier.2 = bf16[2,64,5,3,8,128]{5,4,3,2,1,0:T(8,128)(2,1)} custom-call(s32[1,640]{1,0:T(1,128)} %reshape.26.orders_ref, bf16[2,5,256,1280]{3,2,1,0:T(8,128)(2,1)} %bitcast.16), custom_call_target="tpu_custom_call" | custom-call | flops 5033164800 | bytes 10485760 | tf_op jit(solution)/shard_map/fourier/pallas_call | solution.py:105
  39.0 20.3 %all-to-all-done.1 = bf16[128,5,2,8,128]{4,3,2,1,0:T(8,128)(2,1)S(1)} async-done(((bf16[128,5,2,8,128]{4,3,2,1,0:T(8,128)(2,1)}), bf16[128,5,2,8,128]{4,3,2,1,0:T(8,128)(2,1)S(1)}, u32[]{:S(2)}, u32[]{:S(2)}) %all-to-all-start.1) | async-done | bytes 2621472 | tf_op jit(solution)/shard_map/all_to_all | solution.py:307
  59.3 0.0 copy-start
  59.3 1.5 copy-done
  60.8 8.0 %all-to-all-start = ((bf16[128,5,3,8,128]{4,3,2,1,0:T(8,128)(2,1)}), bf16[128,5,3,8,128]{4,3,2,1,0:T(8,128)(2,1)}, u32[]{:S(2)}, u32[]{:S(2)}) async-start(bf16[128,5,3,8,128]{4,3,2,1,0:T(8,128)(2,1)} %bitcast.13), calls=%async_computation | async-start | bytes 7864320 | tf_op jit(solution)/shard_map/all_to_all | solution.py:307
  68.8 7.6 %copy.9 = bf16[5,2,640,641]{2,3,1,0:T(8,128)(2,1)} copy(bf16[5,2,640,641]{2,1,3,0:T(2,128)(2,1)} %param.5) | data formatting | bytes 16409600 | tf_op args[2]
  76.4 7.3 %pad.4.basis_ref = bf16[5,2,656,640]{3,2,1,0:T(8,128)(2,1)} pad(bf16[5,2,641,640]{3,2,1,0:T(8,128)(2,1)} %bitcast.11, bf16[]{:T(256)} %constant.1.clone.1), padding=0_0x0_0x0_15x0_0 | pad | bytes 16601602 | tf_op jit(solution)/shard_map/jit(_pad)/pad | solution.py:328
  83.7 7.8 %legendre.2 = (bf16[5,2,656,256]{3,2,1,0:T(8,128)(2,1)}, bf16[5,2,656,256]{3,2,1,0:T(8,128)(2,1)}, f32[256,256]{1,0:T(8,128)}) custom-call(bf16[640,2,8,128]{3,2,1,0:T(8,128)(2,1)} %bitcast.12, bf16[5,2,656,640]{3,2,1,0:T(8,128)(2,1)} %pad.4.basis_ref), custom_call_target="tpu_custom_call" | custom-call | flops 2751463424 | bytes 8667136 | tf_op jit(solution)/shard_map/legendre/pallas_call | solution.py:168
  91.4 25.4 %all-to-all-done = bf16[128,5,3,8,128]{4,3,2,1,0:T(8,128)(2,1)} async-done(((bf16[128,5,3,8,128]{4,3,2,1,0:T(8,128)(2,1)}), bf16[128,5,3,8,128]{4,3,2,1,0:T(8,128)(2,1)}, u32[]{:S(2)}, u32[]{:S(2)}) %all-to-all-start) | async-done | bytes 3932192 | tf_op jit(solution)/shard_map/all_to_all | solution.py:307
  116.8 10.1 %legendre.3 = (bf16[5,2,656,256]{3,2,1,0:T(8,128)(2,1)}, bf16[5,2,656,256]{3,2,1,0:T(8,128)(2,1)}, f32[256,256]{1,0:T(8,128)}) custom-call(bf16[640,3,8,128]{3,2,1,0:T(8,128)(2,1)} %bitcast.2.spectra_ref, bf16[5,2,656,640]{3,2,1,0:T(8,128)(2,1)} %pad.4.basis_ref, ...), custom_call_target="tpu_custom_call", output_to_operand_aliasing={{0}: (2, {}), {1}: (3, {})} | custom-call | flops 4127195136 | bytes 13000704 | tf_op jit(solution)/shard_map/legendre/pallas_call | solution.py:168
  126.9 1.1 reshape.31
  128.0 24.4 %all_to_all.20 = f32[128,4,128]{2,1,0:T(4,128)S(1)} all-to-all(f32[128,4,128]{2,1,0:T(4,128)S(1)} %reshape.31), channel_id=1, replica_groups=mesh['grp'=2,'band'=64] {'grp','band'}, dimensions={0} | all-to-all | bytes 524288 | tf_op jit(solution)/shard_map/all_to_all | solution.py:307
  152.4 0.1 reduce_sum.9
  152.6 15.0 %all_to_all.21 = f32[128,4,128]{2,1,0:T(4,128)S(1)} all-to-all(f32[128,4,128]{2,1,0:T(4,128)S(1)} %broadcast_in_dim.4), channel_id=1, replica_groups=mesh['grp'=2,'band'=64] {'grp','band'}, dimensions={0} | all-to-all | bytes 524288 | tf_op jit(solution)/shard_map/all_to_all | solution.py:307
  167.6 0.8 reshape.32.gram_ref
  168.5 29.7 %finish.1 = (bf16[5,641,2,256]{3,2,1,0:T(2,128)(2,1)}, f32[256,256]{1,0:T(8,128)}) custom-call(f32[256,256]{1,0:T(8,128)} %reshape.32.gram_ref, bf16[5,2,656,256]{3,2,1,0:T(8,128)(2,1)} %get-tuple-element.14.high_ref, bf16[5,2,656,256]{3,2,1,0:T(8,128)(2,1)} %get-tuple-element.15.low_ref), custom_call_target="tpu_custom_call" | custom-call | tf_op jit(solution)/shard_map/finish/pallas_call | solution.py:287
  (1 shorter events, 0.0 us)
Async XLA Ops:
  13.7 45.7 %all-to-all-start.1 = ((bf16[128,5,2,8,128]{4,3,2,1,0:T(8,128)(2,1)}), bf16[128,5,2,8,128]{4,3,2,1,0:T(8,128)(2,1)S(1)}, u32[]{:S(2)}, u32[]{:S(2)}) async-start(bf16[128,5,2,8,128]{4,3,2,1,0:T(8,128)(2,1)} %bitcast.14), calls=%async_computation.1 | async-start | bytes 5242880 | tf_op jit(solution)/shard_map/all_to_all | solution.py:307
  59.3 1.5 copy-start
  60.8 56.0 %all-to-all-start = ((bf16[128,5,3,8,128]{4,3,2,1,0:T(8,128)(2,1)}), bf16[128,5,3,8,128]{4,3,2,1,0:T(8,128)(2,1)}, u32[]{:S(2)}, u32[]{:S(2)}) async-start(bf16[128,5,3,8,128]{4,3,2,1,0:T(8,128)(2,1)} %bitcast.13), calls=%async_computation | async-start | bytes 7864320 | tf_op jit(solution)/shard_map/all_to_all | solution.py:307

commit v3 on v2

--- a/solution.py
+++ b/solution.py
@@ -11,7 +11,7 @@
 F32 = jnp.float32
 BF16 = jnp.bfloat16
 AXES = ("grp", "band")
-CHUNKS = (2, 3)
+CHUNKS = (1, 4)
 
 
 def cos_sin_quarter(position, lon_count):
@@ -39,7 +39,7 @@
     step_rows = 32
     half_blocks = lon_count // lanes // 2
     rows = table_ref.shape[0] // pairs
-    orders = orders_ref[...].astype(F32)
+    orders = orders_ref[...].astype(F32).reshape(1, -1)
     high = jnp.floor((orders + 0.5) * (1.0 / 32))
     low = orders - 32.0 * high
     high = jnp.broadcast_to(high, (lanes, high.shape[1])).astype(BF16)
@@ -78,24 +78,24 @@
 def fourier_kernel(chunk, pairs_total, orders_ref, field_ref, out_ref, wave_ref, table_ref):
     lon_count = field_ref.shape[3]
 
-    @pl.when((pl.program_id(0) == 0) & (pl.program_id(1) == 0))
+    @pl.when(pl.program_id(0) == 0)
     def _():
         build_table(chunk, pairs_total, orders_ref, wave_ref, table_ref, lon_count)
 
-    field = field_ref[0, 0]
     pairs = chunk[1]
     rows = table_ref.shape[0] // pairs
-    for pair in range(pairs):
-        result = lax.dot_general(
-            table_ref[pair * rows:(pair + 1) * rows, :], field, (((1,), (1,)), ((), ())), preferred_element_type=F32
-        )
-        left = result[:, :128].reshape(rows // 8, 8, 128)
-        right = result[:, 128:].reshape(rows // 8, 8, 128)
-        low = lax.broadcasted_iota(jnp.int32, left.shape, 1) < 4
-        even = jnp.where(low, left, pltpu.roll(right, 4, 1))
-        odd = jnp.where(low, pltpu.roll(left, 4, 1), right)
-        mixed = jnp.stack([even, odd], axis=1).reshape(rows // 4, 8, 128)
-        out_ref[0, :, 0, pair] = mixed.astype(BF16)
+    for level in range(field_ref.shape[0]):
+        field = field_ref[level, 0]
+        whole = lax.dot_general(table_ref[...], field, (((1,), (1,)), ((), ())), preferred_element_type=F32)
+        for pair in range(pairs):
+            result = whole[pair * rows:(pair + 1) * rows]
+            left = result[:, :128].reshape(rows // 8, 8, 128)
+            right = result[:, 128:].reshape(rows // 8, 8, 128)
+            low = lax.broadcasted_iota(jnp.int32, left.shape, 1) < 4
+            even = jnp.where(low, left, pltpu.roll(right, 4, 1))
+            odd = jnp.where(low, pltpu.roll(left, 4, 1), right)
+            mixed = jnp.stack([even, odd], axis=1).reshape(rows // 4, 8, 128)
+            out_ref[level, :, 0, pair] = mixed.astype(BF16)
 
 
 def transform(fields, orders, bands, pairs_total, chunk):
@@ -104,12 +104,12 @@
     rows = pairs * bands * 4
     return pl.pallas_call(
         functools.partial(fourier_kernel, chunk, pairs_total),
-        grid=(levels, lats),
+        grid=(lats,),
         in_specs=[
-            pl.BlockSpec(orders.shape, lambda l, i: (0, 0)),
-            pl.BlockSpec((1, 1, times, lon_count), lambda l, i: (l, i, 0, 0)),
+            pl.BlockSpec(orders.shape, lambda i: (0,)),
+            pl.BlockSpec((levels, 1, times, lon_count), lambda i: (0, i, 0, 0)),
         ],
-        out_specs=pl.BlockSpec((1, bands, 1, pairs, 8, 128), lambda l, i: (l, 0, i, 0, 0, 0)),
+        out_specs=pl.BlockSpec((levels, bands, 1, pairs, 8, 128), lambda i: (0, 0, i, 0, 0, 0)),
         out_shape=jax.ShapeDtypeStruct((levels, bands, lats, pairs, 8, 128), BF16),
         scratch_shapes=[pltpu.VMEM((rows, 128), F32), pltpu.VMEM((rows, lon_count), BF16)],
         cost_estimate=pl.CostEstimate(
@@ -189,7 +189,7 @@
     )(spectra, legendre, *(carried or ()))
 
 
-def factor_block(groups):
+def factor_block(groups, width):
     count = len(groups)
     n = count * 8
     shape = (8, n)
@@ -197,34 +197,51 @@
     sub = lax.broadcasted_iota(jnp.int32, shape, 0)
     work = list(groups)
     upper, inverse = [jnp.zeros(shape, F32)] * count, [jnp.zeros(shape, F32)] * count
-    for j in range(0, n, 2):
+    for j in range(0, n, width):
         g, r = divmod(j, 8)
-        col0 = [jnp.broadcast_to(work[k][:, j:j + 1], shape) for k in range(g, count)]
-        col1 = [jnp.broadcast_to(work[k][:, j + 1:j + 2], shape) for k in range(g, count)]
-        p = jnp.broadcast_to(col0[0][r:r + 1], shape)
-        q = jnp.broadcast_to(col0[0][r + 1:r + 2], shape)
-        s = jnp.broadcast_to(col1[0][r + 1:r + 2], shape)
-        row0 = jnp.broadcast_to(work[g][r:r + 1], shape)
-        row1 = jnp.broadcast_to(work[g][r + 1:r + 2], shape)
-        over0 = 1.0 / p
-        ratio = q * over0
-        rest = s - q * ratio
-        over1 = 1.0 / rest
-        first, second = lane == j, lane == j + 1
-        unit0 = jnp.where(first, 1.0, jnp.where(second, 0.0, row0))
-        unit1 = jnp.where(second, 1.0, jnp.where(first, 0.0, row1)) - ratio * unit0
-        down0, down1 = unit0 * over0, unit1 * over1
-        pair = first | second
+        inside = (lane >= j) & (lane < j + width)
+        cols = [
+            [jnp.broadcast_to(work[k][:, j + a:j + a + 1], shape) for a in range(width)] for k in range(g, count)
+        ]
+        unit, plain, pivot, over, ratio = [], [], [], [], {}
+        entry = {
+            (b, a): jnp.broadcast_to(cols[0][a][r + b:r + b + 1], shape) for a in range(width) for b in range(a, width)
+        }
+        for a in range(width):
+            pivot.append(entry[a, a])
+            over.append(1.0 / pivot[a])
+            for b in range(a + 1, width):
+                ratio[b, a] = entry[b, a] * over[a]
+            for b in range(a + 1, width):
+                for e in range(b, width):
+                    entry[e, b] = entry[e, b] - ratio[e, a] * entry[b, a]
+        for a in range(width):
+            row = jnp.broadcast_to(work[g][r + a:r + a + 1], shape)
+            start = jnp.where(inside, jnp.where(lane == j + a, 1.0, 0.0), row)
+            for b in range(a):
+                row = row - ratio[a, b] * plain[b]
+                start = start - ratio[a, b] * unit[b]
+            plain.append(row)
+            unit.append(start)
+        down = [unit[a] * over[a] for a in range(width)]
         for k in range(g, count):
-            moved = jnp.where(pair, 0.0, work[k]) - col0[k - g] * down0 - (col1[k - g] - ratio * col0[k - g]) * down1
-            work[k] = moved if k > g else jnp.where(sub > r + 1, moved, work[k])
-        root0, root1 = lax.rsqrt(p), lax.rsqrt(rest)
-        up0 = jnp.where(lane >= j, row0, 0.0) * root0
-        up1 = jnp.where(lane >= j + 1, row1 - ratio * row0, 0.0) * root1
-        inv0 = jnp.where(lane <= j, unit0, 0.0) * root0
-        inv1 = jnp.where(lane <= j + 1, unit1, 0.0) * root1
-        upper[g] = jnp.where(sub == r, up0, jnp.where(sub == r + 1, up1, upper[g]))
-        inverse[g] = jnp.where(sub == r, inv0, jnp.where(sub == r + 1, inv1, inverse[g]))
+            if k == g and r + width == 8:
+                continue
+            moved = jnp.where(inside, 0.0, work[k])
+            reduced = []
+            for a in range(width):
+                value = cols[k - g][a]
+                for b in range(a):
+                    value = value - ratio[a, b] * reduced[b]
+                reduced.append(value)
+                moved = moved - value * down[a]
+            work[k] = moved if k > g else jnp.where(sub >= r + width, moved, work[k])
+        for a in range(width):
+            root = lax.rsqrt(pivot[a])
+            up = jnp.where(lane >= j + a, plain[a], 0.0) * root
+            inv = jnp.where(lane <= j + a, unit[a], 0.0) * root
+            upper[g] = jnp.where(sub == r + a, up, upper[g])
+            inverse[g] = jnp.where(sub == r + a, inv, inverse[g])
     return jnp.concatenate(upper, 0), jnp.concatenate(inverse, 0)
 
 
@@ -238,7 +255,7 @@
     block_ref[...] = gram_ref[:half, :half] * scale
 
     def step(index, carry):
-        upper, inverse = factor_block([block_ref[k * 8:(k + 1) * 8, :] for k in range(half // 8)])
+        upper, inverse = factor_block([block_ref[k * 8:(k + 1) * 8, :] for k in range(half // 8)], 8)
 
         @pl.when(index == 0)
         def _():
@@ -262,32 +279,46 @@
     inverse_ref[:half, half:] = jnp.zeros((half, half), F32)
 
 
-def finish_kernel(scale, gram_ref, high_ref, low_ref, out_ref, factor_ref, inverse_ref, block_ref, top_ref, rest_ref):
-    @pl.when(pl.program_id(0) == 0)
+def finish_kernel(
+    scale, gram_ref, high_any, low_any, out_ref, factor_ref, inverse_ref, block_ref, top_ref, rest_ref, part_ref, sems
+):
+    pair = pl.program_id(0)
+    pairs = part_ref.shape[1]
+
+    def fetch(side, index):
+        source = low_any if side else high_any
+        return pltpu.make_async_copy(source.at[index], part_ref.at[side, index], sems.at[side, index])
+
+    @pl.when(pair == 0)
     def _():
+        for index in range(pairs):
+            fetch(0, index).start()
+            fetch(1, index).start()
         factor_into(scale, gram_ref, factor_ref, inverse_ref, block_ref)
         inverse = inverse_ref[...]
         top = inverse.astype(BF16)
         top_ref[...] = top
         rest_ref[...] = (inverse - top.astype(F32)).astype(BF16)
 
-    rows = out_ref.shape[1]
+    fetch(0, pair).wait()
+    fetch(1, pair).wait()
     across = (((1,), (1,)), ((), ()))
     for c in range(2):
-        value = lax.dot_general(high_ref[0, c], top_ref[...], across, preferred_element_type=F32)
-        value += lax.dot_general(high_ref[0, c], rest_ref[...], across, preferred_element_type=F32)
-        value += lax.dot_general(low_ref[0, c], top_ref[...], across, preferred_element_type=F32)
-        out_ref[0, :, c, :] = value[:rows].astype(BF16)
-
-
-def finish(gram, high, low, total_rows, degree_rows):
-    pairs, _, rows, _ = high.shape
-    block = pl.BlockSpec((1, 2, rows, 256), lambda q: (q, 0, 0, 0))
+        high, low = part_ref[0, pair, c], part_ref[1, pair, c]
+        value = lax.dot_general(high, top_ref[...], across, preferred_element_type=F32)
+        value += lax.dot_general(high, rest_ref[...], across, preferred_element_type=F32)
+        value += lax.dot_general(low, top_ref[...], across, preferred_element_type=F32)
+        out_ref[0, :, c, :] = value.astype(BF16)
+
+
+def finish(gram, high, low, total_rows):
+    pairs, _, degree_rows, _ = high.shape
+    kept = pl.BlockSpec(memory_space=pl.ANY)
     whole = pl.BlockSpec((256, 256), lambda q: (0, 0))
     return pl.pallas_call(
         functools.partial(finish_kernel, 1.0 / total_rows),
         grid=(pairs,),
-        in_specs=[whole, block, block],
+        in_specs=[whole, kept, kept],
         out_specs=[pl.BlockSpec((1, degree_rows, 2, 256), lambda q: (q, 0, 0, 0)), whole],
         out_shape=[
             jax.ShapeDtypeStruct((pairs, degree_rows, 2, 256), BF16),
@@ -298,6 +329,8 @@
             pltpu.VMEM((128, 128), F32),
             pltpu.VMEM((256, 256), BF16),
             pltpu.VMEM((256, 256), BF16),
+            pltpu.VMEM((2, pairs, 2, degree_rows, 256), BF16),
+            pltpu.SemaphoreType.DMA((2, pairs)),
         ],
         name="finish",
     )(gram, high, low)
@@ -317,21 +350,20 @@
     levels, times, lats, lon_count = fields.shape
     groups, bands = lax.axis_size("grp"), lax.axis_size("band")
     pairs, _, lat_total, degree_rows = basis.shape
-    padded_rows = -(-degree_rows // 16) * 16
     fields = fields.transpose(0, 2, 1, 3)
-    orders = wave_order.reshape(1, -1)
+    orders = wave_order
     starts = [sum(CHUNKS[:n]) for n in range(len(CHUNKS))]
     received = []
     for chunk in zip(starts, CHUNKS):
         sent = transform(fields, orders, bands, pairs, chunk)
         received.append(exchange(sent.reshape(groups * bands, lats, chunk[1], 8, 128)))
-    legendre = jnp.pad(basis.transpose(0, 1, 3, 2), ((0, 0), (0, 0), (0, padded_rows - degree_rows), (0, 0)))
+    legendre = basis.transpose(0, 1, 3, 2)
     carried = None
     for start, spectra in zip(starts, received):
         carried = project(spectra.reshape(lat_total, -1, 8, 128), legendre, start, carried)
     high, low, local_gram = carried
     gram = reduce_gram(local_gram, groups * bands)
-    whitened, factor = finish(gram, high, low, levels * pairs * bands * 2 * degree_rows, degree_rows)
+    whitened, factor = finish(gram, high, low, levels * pairs * bands * 2 * degree_rows)
     return (whitened.transpose(0, 2, 1, 3)[None], factor)
 
 

time: 199 us -> 183 us (0.920)
  Pallas kernels: 73.2 us -> 57.4 us
  waiting for transfers between devices: 45.7 us -> 56.9 us
  local copies, waits for them, and re-layouts: 19.6 us -> 10.6 us
    all_to_all x2, waiting for transfers between devices: 45.7 us -> 56.9 us  [exchange(): return lax.all_to_all(value, AXES, split_axis=0, concat_axis=0, tiled=True)]
    pallas_call x1, Pallas kernels: 29.7 us -> 18.9 us  [finish(): pl.pallas_call(functools.partial(finish_kernel, 1.0 / total_rows), grid=(...]
    pad x1 -> x0, local copies, waits for them, and re-layouts: 7.3 us -> none  [shards(): jnp.pad(basis.transpose(0, 1, 3, 2), ((0, 0), (0, 0), (0, padded_rows - d...]
    pallas_call x2, Pallas kernels: 25.6 us -> 21.2 us  [transform(): pl.pallas_call(functools.partial(fourier_kernel, chunk, pairs_total), gri...]
  transfers between devices with their start and end apart: 2 -> 2, of which waited for: 2 -> 2; matrix products, arithmetic and copies ran while one was open for 8% -> 4% of each run, Pallas kernels for 11% -> 10%
where the time goes in v3:
time: 183 us; the launch traced here: 182 us
  Pallas kernels  57.4 us (31%)
  waiting for transfers between devices  56.9 us (31%)
  blocking collectives  38.3 us (21%)
  starting transfers between devices  17.8 us (10%)
  local copies, waits for them, and re-layouts  10.6 us (6%)
    all_to_all x2, waiting for transfers between devices, exchange(): return lax.all_to_all(value, AXES, split_axis=0, concat_axis=0, tiled=True)  56.9 us
    all_to_all x2, blocking collectives, exchange(): return lax.all_to_all(value, AXES, split_axis=0, concat_axis=0, tiled=True)  38.3 us
    pallas_call x2, Pallas kernels, transform(): pl.pallas_call(functools.partial(fourier_kernel, chunk, pairs_total), gri...  21.2 us
    pallas_call x1, Pallas kernels, finish(): pl.pallas_call(functools.partial(finish_kernel, 1.0 / total_rows), grid=(...  18.9 us
    all_to_all x2, starting transfers between devices, exchange(): return lax.all_to_all(value, AXES, split_axis=0, concat_axis=0, tiled=True)  17.8 us
    pallas_call x2, Pallas kernels, project(): pl.pallas_call(functools.partial(legendre_kernel, later), grid=(pairs,),...  17.4 us
    unnamed x3, local copies, waits for them, and re-layouts  8.64 us
  transfers between devices with their start and end apart: 2, of which 2 were waited for; matrix products, arithmetic and copies ran while one was open for 4% of the time, Pallas kernels for 10%

profile of v3, /device:TPU:1, one launch (start us, length us, event | category | flops | bytes accessed | tf_op | source)
XLA Modules:
  0.0 182.0 jit_solution(13562080856214721459)
XLA Ops:
  0.6 7.5 %fourier.3 = bf16[2,64,5,1,8,128]{5,4,3,2,1,0:T(8,128)(2,1)} custom-call(s32[640]{0:T(1024)} %orders_ref.3, bf16[2,5,256,1280]{3,2,1,0:T(8,128)(2,1)} %bitcast.15), custom_call_target="tpu_custom_call" | custom-call | flops 1677721600 | bytes 7864320 | tf_op jit(solution)/shard_map/fourier/pallas_call | solution.py:105
  8.1 11.5 %all-to-all-start.1 = ((bf16[128,5,1,8,128]{4,3,1,2,0:T(8,128)(2,1)}), bf16[128,5,1,8,128]{4,3,1,2,0:T(8,128)(2,1)S(1)}, u32[]{:S(2)}, u32[]{:S(2)}) async-start(bf16[128,5,1,8,128]{4,3,1,2,0:T(8,128)(2,1)} %bitcast.17), calls=%async_computation.1 | async-start | bytes 2621440 | tf_op jit(solution)/shard_map/all_to_all | solution.py:340
  19.6 13.7 %fourier.2 = bf16[2,64,5,4,8,128]{5,4,3,2,1,0:T(8,128)(2,1)} custom-call(s32[640]{0:T(1024)} %orders_ref.3, bf16[2,5,256,1280]{3,2,1,0:T(8,128)(2,1)} %bitcast.16), custom_call_target="tpu_custom_call" | custom-call | flops 6710886400 | bytes 11796480 | tf_op jit(solution)/shard_map/fourier/pallas_call | solution.py:105
  33.3 6.6 %all-to-all-done.1 = bf16[128,5,1,8,128]{4,3,1,2,0:T(8,128)(2,1)S(1)} async-done(((bf16[128,5,1,8,128]{4,3,1,2,0:T(8,128)(2,1)}), bf16[128,5,1,8,128]{4,3,1,2,0:T(8,128)(2,1)S(1)}, u32[]{:S(2)}, u32[]{:S(2)}) %all-to-all-start.1) | async-done | bytes 1310752 | tf_op jit(solution)/shard_map/all_to_all | solution.py:340
  39.8 0.0 copy-start
  39.8 1.1 copy-done
  40.9 6.3 %all-to-all-start = ((bf16[128,5,4,8,128]{4,3,2,1,0:T(8,128)(2,1)}), bf16[128,5,4,8,128]{4,3,2,1,0:T(8,128)(2,1)}, u32[]{:S(2)}, u32[]{:S(2)}) async-start(bf16[128,5,4,8,128]{4,3,2,1,0:T(8,128)(2,1)} %bitcast.18), calls=%async_computation | async-start | bytes 10485760 | tf_op jit(solution)/shard_map/all_to_all | solution.py:340
  47.2 7.6 %copy.11 = bf16[5,2,640,641]{2,3,1,0:T(8,128)(2,1)} copy(bf16[5,2,640,641]{2,1,3,0:T(2,128)(2,1)} %param.5) | data formatting | bytes 16409600 | tf_op args[2]
  54.8 5.0 %legendre.2 = (bf16[5,2,641,256]{3,2,1,0:T(8,128)(2,1)}, bf16[5,2,641,256]{3,2,1,0:T(8,128)(2,1)}, f32[256,256]{1,0:T(8,128)}) custom-call(bf16[640,1,8,128]{3,2,1,0:T(8,128)(2,1)} %bitcast.19, bf16[5,2,641,640]{3,2,1,0:T(8,128)(2,1)} %bitcast.13), custom_call_target="tpu_custom_call" | custom-call | flops 1344274432 | bytes 4264448 | tf_op jit(solution)/shard_map/legendre/pallas_call | solution.py:168
  59.7 50.4 %all-to-all-done = bf16[128,5,4,8,128]{4,3,2,1,0:T(8,128)(2,1)} async-done(((bf16[128,5,4,8,128]{4,3,2,1,0:T(8,128)(2,1)}), bf16[128,5,4,8,128]{4,3,2,1,0:T(8,128)(2,1)}, u32[]{:S(2)}, u32[]{:S(2)}) %all-to-all-start) | async-done | bytes 5242912 | tf_op jit(solution)/shard_map/all_to_all | solution.py:340
  110.1 12.5 %legendre.3 = (bf16[5,2,641,256]{3,2,1,0:T(8,128)(2,1)}, bf16[5,2,641,256]{3,2,1,0:T(8,128)(2,1)}, f32[256,256]{1,0:T(8,128)}) custom-call(bf16[640,4,8,128]{3,2,1,0:T(8,128)(2,1)} %bitcast.2.spectra_ref, bf16[5,2,641,640]{3,2,1,0:T(8,128)(2,1)} %bitcast.14, ...), custom_call_target="tpu_custom_call", output_to_operand_aliasing={{0}: (2, {}), {1}: (3, {})} | custom-call | flops 5377097728 | bytes 17057792 | tf_op jit(solution)/shard_map/legendre/pallas_call | solution.py:168
  122.6 1.1 reshape.27
  123.7 23.3 %all_to_all.20 = f32[128,4,128]{2,1,0:T(4,128)S(1)} all-to-all(f32[128,4,128]{2,1,0:T(4,128)S(1)} %reshape.27), channel_id=1, replica_groups=mesh['grp'=2,'band'=64] {'grp','band'}, dimensions={0} | all-to-all | bytes 524288 | tf_op jit(solution)/shard_map/all_to_all | solution.py:340
  147.0 0.1 reduce_sum.9
  147.1 15.0 %all_to_all.21 = f32[128,4,128]{2,1,0:T(4,128)S(1)} all-to-all(f32[128,4,128]{2,1,0:T(4,128)S(1)} %broadcast_in_dim.4), channel_id=1, replica_groups=mesh['grp'=2,'band'=64] {'grp','band'}, dimensions={0} | all-to-all | bytes 524288 | tf_op jit(solution)/shard_map/all_to_all | solution.py:340
  162.2 0.8 reshape.28.gram_ref
  163.0 18.9 %finish.1 = (bf16[5,641,2,256]{3,2,1,0:T(2,128)(2,1)}, f32[256,256]{1,0:T(8,128)}) custom-call(f32[256,256]{1,0:T(8,128)} %reshape.28.gram_ref, bf16[5,2,641,256]{3,2,1,0:T(8,128)(2,1)} %get-tuple-element.14.high_any, bf16[5,2,641,256]{3,2,1,0:T(8,128)(2,1)} %get-tuple-element.15.low_any), custom_call_target="tpu_custom_call" | custom-call | tf_op jit(solution)/shard_map/finish/pallas_call | solution.py:318
  (1 shorter events, 0.0 us)
Async XLA Ops:
  8.1 31.7 %all-to-all-start.1 = ((bf16[128,5,1,8,128]{4,3,1,2,0:T(8,128)(2,1)}), bf16[128,5,1,8,128]{4,3,1,2,0:T(8,128)(2,1)S(1)}, u32[]{:S(2)}, u32[]{:S(2)}) async-start(bf16[128,5,1,8,128]{4,3,1,2,0:T(8,128)(2,1)} %bitcast.17), calls=%async_computation.1 | async-start | bytes 2621440 | tf_op jit(solution)/shard_map/all_to_all | solution.py:340
  39.8 1.1 copy-start
  40.9 69.2 %all-to-all-start = ((bf16[128,5,4,8,128]{4,3,2,1,0:T(8,128)(2,1)}), bf16[128,5,4,8,128]{4,3,2,1,0:T(8,128)(2,1)}, u32[]{:S(2)}, u32[]{:S(2)}) async-start(bf16[128,5,4,8,128]{4,3,2,1,0:T(8,128)(2,1)} %bitcast.18), calls=%async_computation | async-start | bytes 10485760 | tf_op jit(solution)/shard_map/all_to_all | solution.py:340

commit v4 on v3

--- a/solution.py
+++ b/solution.py
@@ -121,10 +121,10 @@
     )(orders, fields)
 
 
-def legendre_kernel(later, spectra_ref, basis_ref, *refs):
+def legendre_kernel(later, last, spectra_ref, basis_ref, *refs):
     if later:
-        before_ref, refs = refs[2], refs[3:]
-    high_ref, low_ref, gram_ref, wide_ref, side_ref, cross_ref = refs
+        before_ref, refs = refs[1], refs[2:]
+    part_ref, out_ref, wide_ref, side_ref, gram_ref, cross_ref = refs
     step = pl.program_id(0)
 
     @pl.when(step == 0)
@@ -138,51 +138,60 @@
         for h in range(2):
             for c in range(2):
                 piece = wide_ref[pl.ds(half * 4 + h * 2 + c, lats, stride=8), :]
-                side_ref[h, :, c * 256 + half * 128:c * 256 + half * 128 + 128] = piece.astype(BF16)
-    product = jnp.dot(basis_ref[0, 0], side_ref[0], preferred_element_type=F32)
-    product += jnp.dot(basis_ref[0, 1], side_ref[1], preferred_element_type=F32)
+                at = c * 256 + half * 128
+                side_ref[h * lats:(h + 1) * lats, at:at + 128] = piece.astype(BF16)
+    product = jnp.dot(basis_ref[0], side_ref[...], preferred_element_type=F32)
     flip = (((0,), (0,)), ((), ()))
     for c in range(2):
         value = product[:, c * 256:(c + 1) * 256]
         high = value.astype(BF16)
         low = (value - high.astype(F32)).astype(BF16)
-        high_ref[0, c] = high
-        low_ref[0, c] = low
+        part_ref[0, c, :, :256] = high
+        part_ref[0, c, :, 256:] = low
         gram_ref[...] += lax.dot_general(high, high, flip, preferred_element_type=F32)
         gram_ref[...] += lax.dot_general(low, low, flip, preferred_element_type=F32)
         cross_ref[...] += lax.dot_general(high, low, flip, preferred_element_type=F32)
 
     @pl.when(step == pl.num_programs(0) - 1)
     def _():
-        gram_ref[...] += cross_ref[...] + cross_ref[...].T
-
-
-def project(spectra, legendre, start, carried):
+        total = gram_ref[...] + cross_ref[...] + cross_ref[...].T
+        if last:
+            out_ref[...] = jnp.stack([total[:, :128], total[:, 128:]]).reshape(out_ref.shape)
+        else:
+            out_ref[...] = total
+
+
+def project(spectra, legendre, start, carried, last):
     lats, pairs = spectra.shape[:2]
-    pairs_total, _, rows, _ = legendre.shape
-    coefficient = jax.ShapeDtypeStruct((pairs_total, 2, rows, 256), BF16)
-    block = pl.BlockSpec((1, 2, rows, 256), lambda q: (q + start, 0, 0, 0))
+    pairs_total, rows, both = legendre.shape
     whole = pl.BlockSpec((256, 256), lambda q: (0, 0))
     later = carried is not None
-    kept = pl.BlockSpec(memory_space=pl.ANY)
+    pieces = (128, 4, 128) if last else (256, 256)
     return pl.pallas_call(
-        functools.partial(legendre_kernel, later),
+        functools.partial(legendre_kernel, later, last),
         grid=(pairs,),
         in_specs=[
             pl.BlockSpec((lats, 1, 8, 128), lambda q: (0, q, 0, 0)),
-            pl.BlockSpec((1, 2, rows, lats), lambda q: (q + start, 0, 0, 0)),
-        ] + ([kept, kept, whole] if later else []),
-        out_specs=[block, block, whole],
-        out_shape=[coefficient, coefficient, jax.ShapeDtypeStruct((256, 256), F32)],
+            pl.BlockSpec((1, rows, both), lambda q: (q + start, 0, 0)),
+        ] + ([pl.BlockSpec(memory_space=pl.ANY), whole] if later else []),
+        out_specs=[
+            pl.BlockSpec((1, 2, rows, 512), lambda q: (q + start, 0, 0, 0)),
+            pl.BlockSpec(pieces, lambda q: (0,) * len(pieces)),
+        ],
+        out_shape=[
+            jax.ShapeDtypeStruct((pairs_total, 2, rows, 512), BF16),
+            jax.ShapeDtypeStruct(pieces, F32),
+        ],
         scratch_shapes=[
             pltpu.VMEM((lats * 8, 128), F32),
-            pltpu.VMEM((2, lats, 512), BF16),
+            pltpu.VMEM((both, 512), BF16),
             pltpu.VMEM((256, 256), F32),
-        ],
-        input_output_aliases={2: 0, 3: 1} if later else {},
+            pltpu.VMEM((256, 256), F32),
+        ],
+        input_output_aliases={2: 0} if later else {},
         cost_estimate=pl.CostEstimate(
-            flops=pairs * (4 * rows * lats * 512 + 12 * rows * 256 * 256),
-            bytes_accessed=pairs * (lats * 2048 + 4 * rows * lats + rows * 2048),
+            flops=pairs * (2 * rows * both * 512 + 12 * rows * 256 * 256),
+            bytes_accessed=pairs * (lats * 2048 + 2 * rows * both + rows * 2048),
             transcendentals=0,
         ),
         name="legendre",
@@ -280,70 +289,67 @@
 
 
 def finish_kernel(
-    scale, gram_ref, high_any, low_any, out_ref, factor_ref, inverse_ref, block_ref, top_ref, rest_ref, part_ref, sems
+    scale, pieces_ref, part_any, out_ref, factor_ref, gram_ref, inverse_ref, block_ref, weight_ref, part_ref, sems
 ):
     pair = pl.program_id(0)
-    pairs = part_ref.shape[1]
-
-    def fetch(side, index):
-        source = low_any if side else high_any
-        return pltpu.make_async_copy(source.at[index], part_ref.at[side, index], sems.at[side, index])
+
+    def fetch(index):
+        return pltpu.make_async_copy(part_any.at[index], part_ref.at[index], sems.at[index])
 
     @pl.when(pair == 0)
     def _():
-        for index in range(pairs):
-            fetch(0, index).start()
-            fetch(1, index).start()
+        for index in range(part_ref.shape[0]):
+            fetch(index).start()
+        gram_ref[:, :128] = pieces_ref[:64].reshape(256, 128)
+        gram_ref[:, 128:] = pieces_ref[64:].reshape(256, 128)
         factor_into(scale, gram_ref, factor_ref, inverse_ref, block_ref)
-        inverse = inverse_ref[...]
-        top = inverse.astype(BF16)
-        top_ref[...] = top
-        rest_ref[...] = (inverse - top.astype(F32)).astype(BF16)
-
-    fetch(0, pair).wait()
-    fetch(1, pair).wait()
-    across = (((1,), (1,)), ((), ()))
+        turned = inverse_ref[...].T
+        top = turned.astype(BF16)
+        weight_ref[:256] = top
+        weight_ref[256:512] = top
+        weight_ref[512:] = (turned - top.astype(F32)).astype(BF16)
+
+    fetch(pair).wait()
     for c in range(2):
-        high, low = part_ref[0, pair, c], part_ref[1, pair, c]
-        value = lax.dot_general(high, top_ref[...], across, preferred_element_type=F32)
-        value += lax.dot_general(high, rest_ref[...], across, preferred_element_type=F32)
-        value += lax.dot_general(low, top_ref[...], across, preferred_element_type=F32)
+        part = part_ref[pair, c]
+        wide = jnp.concatenate([part, part[:, :256]], axis=1)
+        value = jnp.dot(wide, weight_ref[...], preferred_element_type=F32)
         out_ref[0, :, c, :] = value.astype(BF16)
 
 
-def finish(gram, high, low, total_rows):
-    pairs, _, degree_rows, _ = high.shape
-    kept = pl.BlockSpec(memory_space=pl.ANY)
-    whole = pl.BlockSpec((256, 256), lambda q: (0, 0))
+def finish(pieces, parts, total_rows):
+    pairs, _, degree_rows, _ = parts.shape
     return pl.pallas_call(
         functools.partial(finish_kernel, 1.0 / total_rows),
         grid=(pairs,),
-        in_specs=[whole, kept, kept],
-        out_specs=[pl.BlockSpec((1, degree_rows, 2, 256), lambda q: (q, 0, 0, 0)), whole],
+        in_specs=[pl.BlockSpec(pieces.shape, lambda q: (0, 0, 0)), pl.BlockSpec(memory_space=pl.ANY)],
+        out_specs=[
+            pl.BlockSpec((1, degree_rows, 2, 256), lambda q: (q, 0, 0, 0)),
+            pl.BlockSpec((256, 256), lambda q: (0, 0)),
+        ],
         out_shape=[
             jax.ShapeDtypeStruct((pairs, degree_rows, 2, 256), BF16),
             jax.ShapeDtypeStruct((256, 256), F32),
         ],
         scratch_shapes=[
             pltpu.VMEM((256, 256), F32),
+            pltpu.VMEM((256, 256), F32),
             pltpu.VMEM((128, 128), F32),
-            pltpu.VMEM((256, 256), BF16),
-            pltpu.VMEM((256, 256), BF16),
-            pltpu.VMEM((2, pairs, 2, degree_rows, 256), BF16),
-            pltpu.SemaphoreType.DMA((2, pairs)),
+            pltpu.VMEM((768, 256), BF16),
+            pltpu.VMEM(parts.shape, BF16),
+            pltpu.SemaphoreType.DMA((pairs,)),
         ],
         name="finish",
-    )(gram, high, low)
+    )(pieces, parts)
 
 
 def exchange(value):
     return lax.all_to_all(value, AXES, split_axis=0, concat_axis=0, tiled=True)
 
 
-def reduce_gram(gram, devices):
-    pieces = gram.reshape(devices, -1, 128)
+def reduce_gram(pieces):
     total = exchange(pieces).sum(axis=0, keepdims=True)
-    return exchange(jnp.broadcast_to(total, pieces.shape)).reshape(gram.shape)
+    return exchange(jnp.broadcast_to(total, pieces.shape))
 
 
 def shards(fields, wave_order, basis):
@@ -357,13 +363,13 @@
     for chunk in zip(starts, CHUNKS):
         sent = transform(fields, orders, bands, pairs, chunk)
         received.append(exchange(sent.reshape(groups * bands, lats, chunk[1], 8, 128)))
-    legendre = basis.transpose(0, 1, 3, 2)
+    legendre = basis.transpose(0, 3, 1, 2).reshape(pairs, degree_rows, 2 * lat_total)
     carried = None
     for start, spectra in zip(starts, received):
-        carried = project(spectra.reshape(lat_total, -1, 8, 128), legendre, start, carried)
-    high, low, local_gram = carried
-    gram = reduce_gram(local_gram, groups * bands)
-    whitened, factor = finish(gram, high, low, levels * pairs * bands * 2 * degree_rows)
+        last = start == starts[-1]
+        carried = project(spectra.reshape(lat_total, -1, 8, 128), legendre, start, carried, last)
+    parts, pieces = carried
+    whitened, factor = finish(reduce_gram(pieces), parts, levels * pairs * bands * 2 * degree_rows)
     return (whitened.transpose(0, 2, 1, 3)[None], factor)
 
 

time: 183 us -> 179 us (0.978)
  waiting for transfers between devices: 56.9 us -> 48.1 us
  local copies, waits for them, and re-layouts: 10.6 us -> 16.6 us
    reshape x2 -> x1, local copies, waits for them, and re-layouts: 1.9 us -> 16.6 us  [shards(): basis.transpose(0, 3, 1, 2).reshape(pairs, degree_rows, 2 * lat_total)]
    all_to_all x2, waiting for transfers between devices: 56.9 us -> 48.1 us  [exchange(): return lax.all_to_all(value, AXES, split_axis=0, concat_axis=0, tiled=True)]
    unnamed x3 -> x2, local copies, waits for them, and re-layouts: 8.64 us -> 0.01 us
  transfers between devices with their start and end apart: 2 -> 2, of which waited for: 2 -> 2; matrix products, arithmetic and copies ran while one was open for 4% -> 9% of each run, Pallas kernels for 10% -> 10%
where the time goes in v4:
time: 179 us
  Pallas kernels  56.6 us (32%)
  waiting for transfers between devices  48.1 us (27%)
  blocking collectives  38.6 us (22%)
  starting transfers between devices  17.8 us (10%)
  local copies, waits for them, and re-layouts  16.6 us (9%)
    all_to_all x2, waiting for transfers between devices, exchange(): return lax.all_to_all(value, AXES, split_axis=0, concat_axis=0, tiled=True)  48.1 us
    all_to_all x2, blocking collectives, exchange(): return lax.all_to_all(value, AXES, split_axis=0, concat_axis=0, tiled=True)  38.6 us
    pallas_call x2, Pallas kernels, transform(): pl.pallas_call(functools.partial(fourier_kernel, chunk, pairs_total), gri...  21.2 us
    pallas_call x1, Pallas kernels, finish(): pl.pallas_call(functools.partial(finish_kernel, 1.0 / total_rows), grid=(...  18.7 us
    all_to_all x2, starting transfers between devices, exchange(): return lax.all_to_all(value, AXES, split_axis=0, concat_axis=0, tiled=True)  17.8 us
    pallas_call x2, Pallas kernels, project(): pl.pallas_call(functools.partial(legendre_kernel, later, last), grid=(pai...  16.7 us
    reshape x1, local copies, waits for them, and re-layouts, shards(): basis.transpose(0, 3, 1, 2).reshape(pairs, degree_rows, 2 * lat_total)  16.6 us
  transfers between devices with their start and end apart: 2, of which 2 were waited for; matrix products, arithmetic and copies ran while one was open for 9% of the time, Pallas kernels for 10%

profile of v4, /device:TPU:1, one launch (start us, length us, event | category | flops | bytes accessed | tf_op | source)
XLA Modules:
  0.0 178.7 jit_solution(1538471881900159601)
XLA Ops:
  0.6 7.5 %fourier.3 = bf16[2,64,5,1,8,128]{5,4,3,2,1,0:T(8,128)(2,1)} custom-call(s32[640]{0:T(1024)} %orders_ref.3, bf16[2,5,256,1280]{3,2,1,0:T(8,128)(2,1)} %bitcast.12), custom_call_target="tpu_custom_call" | custom-call | flops 1677721600 | bytes 7864320 | tf_op jit(solution)/shard_map/fourier/pallas_call | solution.py:105
  8.1 11.5 %all-to-all-start.1 = ((bf16[128,5,1,8,128]{4,3,1,2,0:T(8,128)(2,1)}), bf16[128,5,1,8,128]{4,3,1,2,0:T(8,128)(2,1)S(1)}, u32[]{:S(2)}, u32[]{:S(2)}) async-start(bf16[128,5,1,8,128]{4,3,1,2,0:T(8,128)(2,1)} %bitcast.14), calls=%async_computation.1 | async-start | bytes 2621440 | tf_op jit(solution)/shard_map/all_to_all | solution.py:347
  19.6 13.7 %fourier.2 = bf16[2,64,5,4,8,128]{5,4,3,2,1,0:T(8,128)(2,1)} custom-call(s32[640]{0:T(1024)} %orders_ref.3, bf16[2,5,256,1280]{3,2,1,0:T(8,128)(2,1)} %bitcast.13), custom_call_target="tpu_custom_call" | custom-call | flops 6710886400 | bytes 11796480 | tf_op jit(solution)/shard_map/fourier/pallas_call | solution.py:105
  33.3 6.5 %all-to-all-done.1 = bf16[128,5,1,8,128]{4,3,1,2,0:T(8,128)(2,1)S(1)} async-done(((bf16[128,5,1,8,128]{4,3,1,2,0:T(8,128)(2,1)}), bf16[128,5,1,8,128]{4,3,1,2,0:T(8,128)(2,1)S(1)}, u32[]{:S(2)}, u32[]{:S(2)}) %all-to-all-start.1) | async-done | bytes 1310752 | tf_op jit(solution)/shard_map/all_to_all | solution.py:347
  39.8 0.0 copy-start
  39.8 6.3 %all-to-all-start = ((bf16[128,5,4,8,128]{4,3,2,1,0:T(8,128)(2,1)}), bf16[128,5,4,8,128]{4,3,2,1,0:T(8,128)(2,1)}, u32[]{:S(2)}, u32[]{:S(2)}) async-start(bf16[128,5,4,8,128]{4,3,2,1,0:T(8,128)(2,1)} %bitcast.15), calls=%async_computation | async-start | bytes 10485760 | tf_op jit(solution)/shard_map/all_to_all | solution.py:347
  46.1 16.6 %reshape.22.basis_ref = bf16[5,641,1280]{2,1,0:T(8,128)(2,1)} reshape(bf16[5,641,2,640]{3,2,1,0:T(2,128)(2,1)} %bitcast.11) | data formatting | bytes 16409600 | tf_op jit(solution)/shard_map/reshape | solution.py:366
  62.7 0.0 copy-done
  62.7 4.8 %legendre.2 = (bf16[5,2,641,512]{3,2,1,0:T(8,128)(2,1)}, f32[256,256]{1,0:T(8,128)}) custom-call(bf16[640,1,8,128]{3,2,1,0:T(8,128)(2,1)} %bitcast.16, bf16[5,641,1280]{2,1,0:T(8,128)(2,1)} %reshape.22.basis_ref), custom_call_target="tpu_custom_call" | custom-call | flops 1344274432 | bytes 4264448 | tf_op jit(solution)/shard_map/legendre/pallas_call | solution.py:170
  67.5 41.5 %all-to-all-done = bf16[128,5,4,8,128]{4,3,2,1,0:T(8,128)(2,1)} async-done(((bf16[128,5,4,8,128]{4,3,2,1,0:T(8,128)(2,1)}), bf16[128,5,4,8,128]{4,3,2,1,0:T(8,128)(2,1)}, u32[]{:S(2)}, u32[]{:S(2)}) %all-to-all-start) | async-done | bytes 5242912 | tf_op jit(solution)/shard_map/all_to_all | solution.py:347
  109.0 11.9 %legendre.3 = (bf16[5,2,641,512]{3,2,1,0:T(8,128)(2,1)}, f32[128,4,128]{2,1,0:T(4,128)}) custom-call(bf16[640,4,8,128]{3,2,1,0:T(8,128)(2,1)} %bitcast.2.spectra_ref, bf16[5,641,1280]{2,1,0:T(8,128)(2,1)} %reshape.22.basis_ref, bf16[5,2,641,512]{3,2,1,0:T(8,128)(2,1)} %get-tuple-element.8.refs_0_, ...), custom_call_target="tpu_custom_call", output_to_operand_aliasing={{0}: (2, {})} | custom-call | flops 5377097728 | bytes 17057792 | tf_op jit(solution)/shard_map/legendre/pallas_call | solution.py:170
  121.0 23.4 %all_to_all.20 = f32[128,4,128]{2,1,0:T(4,128)S(1)} all-to-all(f32[128,4,128]{2,1,0:T(4,128)} %get-tuple-element.10), channel_id=1, replica_groups=mesh['grp'=2,'band'=64] {'grp','band'}, dimensions={0} | all-to-all | bytes 524288 | tf_op jit(solution)/shard_map/all_to_all | solution.py:347
  144.4 0.1 reduce_sum.9
  144.6 15.2 %all_to_all.21.pieces_ref = f32[128,4,128]{2,1,0:T(4,128)} all-to-all(f32[128,4,128]{2,1,0:T(4,128)S(1)} %broadcast_in_dim.4), channel_id=1, replica_groups=mesh['grp'=2,'band'=64] {'grp','band'}, dimensions={0} | all-to-all | bytes 524288 | tf_op jit(solution)/shard_map/all_to_all | solution.py:347
  159.8 18.7 %finish.1 = (bf16[5,641,2,256]{3,2,1,0:T(2,128)(2,1)}, f32[256,256]{1,0:T(8,128)}) custom-call(f32[128,4,128]{2,1,0:T(4,128)} %all_to_all.21.pieces_ref, bf16[5,2,641,512]{3,2,1,0:T(8,128)(2,1)} %get-tuple-element.11.part_any), custom_call_target="tpu_custom_call" | custom-call | tf_op jit(solution)/shard_map/finish/pallas_call | solution.py:322
  (1 shorter events, 0.0 us)
Async XLA Ops:
  8.1 31.7 %all-to-all-start.1 = ((bf16[128,5,1,8,128]{4,3,1,2,0:T(8,128)(2,1)}), bf16[128,5,1,8,128]{4,3,1,2,0:T(8,128)(2,1)S(1)}, u32[]{:S(2)}, u32[]{:S(2)}) async-start(bf16[128,5,1,8,128]{4,3,1,2,0:T(8,128)(2,1)} %bitcast.14), calls=%async_computation.1 | async-start | bytes 2621440 | tf_op jit(solution)/shard_map/all_to_all | solution.py:347
  39.8 22.9 %copy-start = (bf16[128,5,1,8,128]{4,3,1,2,0:T(8,128)(2,1)}, bf16[128,5,1,8,128]{4,3,1,2,0:T(8,128)(2,1)S(1)}, u32[]{:S(2)}) copy-start(bf16[128,5,1,8,128]{4,3,1,2,0:T(8,128)(2,1)S(1)} %all-to-all-done.1) | copy-start | bytes 3932164
  39.8 69.2 %all-to-all-start = ((bf16[128,5,4,8,128]{4,3,2,1,0:T(8,128)(2,1)}), bf16[128,5,4,8,128]{4,3,2,1,0:T(8,128)(2,1)}, u32[]{:S(2)}, u32[]{:S(2)}) async-start(bf16[128,5,4,8,128]{4,3,2,1,0:T(8,128)(2,1)} %bitcast.15), calls=%async_computation | async-start | bytes 10485760 | tf_op jit(solution)/shard_map/all_to_all | solution.py:347

commit v5 on v4

--- a/solution.py
+++ b/solution.py
@@ -75,43 +75,53 @@
     lax.fori_loop(0, table_ref.shape[0] // step_rows, body, 0)
 
 
-def fourier_kernel(chunk, pairs_total, orders_ref, field_ref, out_ref, wave_ref, table_ref):
-    lon_count = field_ref.shape[3]
-
-    @pl.when(pl.program_id(0) == 0)
-    def _():
-        build_table(chunk, pairs_total, orders_ref, wave_ref, table_ref, lon_count)
-
+def fourier_kernel(chunk, pairs_total, orders_ref, field_any, out_ref, wave_ref, table_ref, field_ref, sems):
+    levels, lats, _, lon_count = field_ref.shape
+
+    def fetch(lat):
+        return pltpu.make_async_copy(field_any.at[:, lat], field_ref.at[:, lat], sems.at[lat])
+
+    for lat in range(lats):
+        fetch(lat).start()
+    build_table(chunk, pairs_total, orders_ref, wave_ref, table_ref, lon_count)
     pairs = chunk[1]
     rows = table_ref.shape[0] // pairs
-    for level in range(field_ref.shape[0]):
-        field = field_ref[level, 0]
-        whole = lax.dot_general(table_ref[...], field, (((1,), (1,)), ((), ())), preferred_element_type=F32)
-        for pair in range(pairs):
-            result = whole[pair * rows:(pair + 1) * rows]
-            left = result[:, :128].reshape(rows // 8, 8, 128)
-            right = result[:, 128:].reshape(rows // 8, 8, 128)
-            low = lax.broadcasted_iota(jnp.int32, left.shape, 1) < 4
-            even = jnp.where(low, left, pltpu.roll(right, 4, 1))
-            odd = jnp.where(low, pltpu.roll(left, 4, 1), right)
-            mixed = jnp.stack([even, odd], axis=1).reshape(rows // 4, 8, 128)
-            out_ref[level, :, 0, pair] = mixed.astype(BF16)
+
+    def body(lat, carry):
+        fetch(lat).wait()
+        for level in range(levels):
+            field = field_ref[level, lat]
+            whole = lax.dot_general(table_ref[...], field, (((1,), (1,)), ((), ())), preferred_element_type=F32)
+            for pair in range(pairs):
+                result = whole[pair * rows:(pair + 1) * rows]
+                left = result[:, :128].reshape(rows // 8, 8, 128)
+                right = result[:, 128:].reshape(rows // 8, 8, 128)
+                low = lax.broadcasted_iota(jnp.int32, left.shape, 1) < 4
+                even = jnp.where(low, left, pltpu.roll(right, 4, 1))
+                odd = jnp.where(low, pltpu.roll(left, 4, 1), right)
+                mixed = jnp.stack([even, odd], axis=1).reshape(rows // 4, 8, 128)
+                out_ref[level, :, lat, pair] = mixed.astype(BF16)
+        return carry
+
+    lax.fori_loop(0, lats, body, 0)
 
 
 def transform(fields, orders, bands, pairs_total, chunk):
     levels, lats, times, lon_count = fields.shape
     pairs = chunk[1]
     rows = pairs * bands * 4
+    near = pl.BlockSpec(memory_space=pltpu.VMEM)
     return pl.pallas_call(
         functools.partial(fourier_kernel, chunk, pairs_total),
-        grid=(lats,),
-        in_specs=[
-            pl.BlockSpec(orders.shape, lambda i: (0,)),
-            pl.BlockSpec((levels, 1, times, lon_count), lambda i: (0, i, 0, 0)),
-        ],
-        out_specs=pl.BlockSpec((levels, bands, 1, pairs, 8, 128), lambda i: (0, 0, i, 0, 0, 0)),
+        in_specs=[near, pl.BlockSpec(memory_space=pl.ANY)],
+        out_specs=near,
         out_shape=jax.ShapeDtypeStruct((levels, bands, lats, pairs, 8, 128), BF16),
-        scratch_shapes=[pltpu.VMEM((rows, 128), F32), pltpu.VMEM((rows, lon_count), BF16)],
+        scratch_shapes=[
+            pltpu.VMEM((rows, 128), F32),
+            pltpu.VMEM((rows, lon_count), BF16),
+            pltpu.VMEM(fields.shape, BF16),
+            pltpu.SemaphoreType.DMA((lats,)),
+        ],
         cost_estimate=pl.CostEstimate(
             flops=2 * rows * levels * lats * times * lon_count,
             bytes_accessed=2 * levels * lats * times * (lon_count + rows),

time: 179 us -> 178 us (level)
  transfers between devices with their start and end apart: 2 -> 2, of which waited for: 2 -> 2; matrix products, arithmetic and copies ran while one was open for 9% -> 9% of each run, Pallas kernels for 10% -> 11%
where the time goes in v5:
time: 178 us; the launch traced here: 177 us
  Pallas kernels  55.2 us (31%)
  waiting for transfers between devices  47.7 us (27%)
  blocking collectives  38.6 us (22%)
  starting transfers between devices  17.8 us (10%)
  local copies, waits for them, and re-layouts  16.6 us (9%)
    all_to_all x2, waiting for transfers between devices, exchange(): return lax.all_to_all(value, AXES, split_axis=0, concat_axis=0, tiled=True)  47.7 us
    all_to_all x2, blocking collectives, exchange(): return lax.all_to_all(value, AXES, split_axis=0, concat_axis=0, tiled=True)  38.6 us
    pallas_call x2, Pallas kernels, transform(): pl.pallas_call(functools.partial(fourier_kernel, chunk, pairs_total), in_...  19.8 us
    pallas_call x1, Pallas kernels, finish(): pl.pallas_call(functools.partial(finish_kernel, 1.0 / total_rows), grid=(...  18.7 us
    all_to_all x2, starting transfers between devices, exchange(): return lax.all_to_all(value, AXES, split_axis=0, concat_axis=0, tiled=True)  17.8 us
    pallas_call x2, Pallas kernels, project(): pl.pallas_call(functools.partial(legendre_kernel, later, last), grid=(pai...  16.7 us
    reshape x1, local copies, waits for them, and re-layouts, shards(): basis.transpose(0, 3, 1, 2).reshape(pairs, degree_rows, 2 * lat_total)  16.6 us
  transfers between devices with their start and end apart: 2, of which 2 were waited for; matrix products, arithmetic and copies ran while one was open for 9% of the time, Pallas kernels for 11%

profile of v5, /device:TPU:1, one launch (start us, length us, event | category | flops | bytes accessed | tf_op | source)
XLA Modules:
  0.0 177.0 jit_solution(17901561333345257738)
XLA Ops:
  0.6 5.8 %fourier.3 = bf16[2,64,5,1,8,128]{5,4,3,2,1,0:T(8,128)(2,1)} custom-call(s32[640]{0:T(1024)} %orders_ref.3, bf16[2,5,256,1280]{3,2,1,0:T(8,128)(2,1)} %bitcast.12), custom_call_target="tpu_custom_call" | custom-call | flops 1677721600 | bytes 7864320 | tf_op jit(solution)/shard_map/fourier/pallas_call | solution.py:114
  6.4 11.5 %all-to-all-start.1 = ((bf16[128,5,1,8,128]{4,3,1,2,0:T(8,128)(2,1)}), bf16[128,5,1,8,128]{4,3,1,2,0:T(8,128)(2,1)S(1)}, u32[]{:S(2)}, u32[]{:S(2)}) async-start(bf16[128,5,1,8,128]{4,3,1,2,0:T(8,128)(2,1)} %bitcast.14), calls=%async_computation.1 | async-start | bytes 2621440 | tf_op jit(solution)/shard_map/all_to_all | solution.py:357
  17.9 14.0 %fourier.2 = bf16[2,64,5,4,8,128]{5,4,3,2,1,0:T(8,128)(2,1)} custom-call(s32[640]{0:T(1024)} %orders_ref.3, bf16[2,5,256,1280]{3,2,1,0:T(8,128)(2,1)} %bitcast.13), custom_call_target="tpu_custom_call" | custom-call | flops 6710886400 | bytes 11796480 | tf_op jit(solution)/shard_map/fourier/pallas_call | solution.py:114
  32.0 6.2 %all-to-all-done.1 = bf16[128,5,1,8,128]{4,3,1,2,0:T(8,128)(2,1)S(1)} async-done(((bf16[128,5,1,8,128]{4,3,1,2,0:T(8,128)(2,1)}), bf16[128,5,1,8,128]{4,3,1,2,0:T(8,128)(2,1)S(1)}, u32[]{:S(2)}, u32[]{:S(2)}) %all-to-all-start.1) | async-done | bytes 1310752 | tf_op jit(solution)/shard_map/all_to_all | solution.py:357
  38.2 0.0 copy-start
  38.2 6.3 %all-to-all-start = ((bf16[128,5,4,8,128]{4,3,2,1,0:T(8,128)(2,1)}), bf16[128,5,4,8,128]{4,3,2,1,0:T(8,128)(2,1)}, u32[]{:S(2)}, u32[]{:S(2)}) async-start(bf16[128,5,4,8,128]{4,3,2,1,0:T(8,128)(2,1)} %bitcast.15), calls=%async_computation | async-start | bytes 10485760 | tf_op jit(solution)/shard_map/all_to_all | solution.py:357
  44.5 16.6 %reshape.22.basis_ref = bf16[5,641,1280]{2,1,0:T(8,128)(2,1)} reshape(bf16[5,641,2,640]{3,2,1,0:T(2,128)(2,1)} %bitcast.11) | data formatting | bytes 16409600 | tf_op jit(solution)/shard_map/reshape | solution.py:376
  61.1 0.0 copy-done
  61.1 4.8 %legendre.2 = (bf16[5,2,641,512]{3,2,1,0:T(8,128)(2,1)}, f32[256,256]{1,0:T(8,128)}) custom-call(bf16[640,1,8,128]{3,2,1,0:T(8,128)(2,1)} %bitcast.16, bf16[5,641,1280]{2,1,0:T(8,128)(2,1)} %reshape.22.basis_ref), custom_call_target="tpu_custom_call" | custom-call | flops 1344274432 | bytes 4264448 | tf_op jit(solution)/shard_map/legendre/pallas_call | solution.py:180
  65.8 41.5 %all-to-all-done = bf16[128,5,4,8,128]{4,3,2,1,0:T(8,128)(2,1)} async-done(((bf16[128,5,4,8,128]{4,3,2,1,0:T(8,128)(2,1)}), bf16[128,5,4,8,128]{4,3,2,1,0:T(8,128)(2,1)}, u32[]{:S(2)}, u32[]{:S(2)}) %all-to-all-start) | async-done | bytes 5242912 | tf_op jit(solution)/shard_map/all_to_all | solution.py:357
  107.4 11.9 %legendre.3 = (bf16[5,2,641,512]{3,2,1,0:T(8,128)(2,1)}, f32[128,4,128]{2,1,0:T(4,128)}) custom-call(bf16[640,4,8,128]{3,2,1,0:T(8,128)(2,1)} %bitcast.2.spectra_ref, bf16[5,641,1280]{2,1,0:T(8,128)(2,1)} %reshape.22.basis_ref, bf16[5,2,641,512]{3,2,1,0:T(8,128)(2,1)} %get-tuple-element.8.refs_0_, ...), custom_call_target="tpu_custom_call", output_to_operand_aliasing={{0}: (2, {})} | custom-call | flops 5377097728 | bytes 17057792 | tf_op jit(solution)/shard_map/legendre/pallas_call | solution.py:180
  119.3 23.4 %all_to_all.20 = f32[128,4,128]{2,1,0:T(4,128)S(1)} all-to-all(f32[128,4,128]{2,1,0:T(4,128)} %get-tuple-element.10), channel_id=1, replica_groups=mesh['grp'=2,'band'=64] {'grp','band'}, dimensions={0} | all-to-all | bytes 524288 | tf_op jit(solution)/shard_map/all_to_all | solution.py:357
  142.7 0.1 reduce_sum.9
  142.9 15.2 %all_to_all.21.pieces_ref = f32[128,4,128]{2,1,0:T(4,128)} all-to-all(f32[128,4,128]{2,1,0:T(4,128)S(1)} %broadcast_in_dim.4), channel_id=1, replica_groups=mesh['grp'=2,'band'=64] {'grp','band'}, dimensions={0} | all-to-all | bytes 524288 | tf_op jit(solution)/shard_map/all_to_all | solution.py:357
  158.1 18.7 %finish.1 = (bf16[5,641,2,256]{3,2,1,0:T(2,128)(2,1)}, f32[256,256]{1,0:T(8,128)}) custom-call(f32[128,4,128]{2,1,0:T(4,128)} %all_to_all.21.pieces_ref, bf16[5,2,641,512]{3,2,1,0:T(8,128)(2,1)} %get-tuple-element.11.part_any), custom_call_target="tpu_custom_call" | custom-call | tf_op jit(solution)/shard_map/finish/pallas_call | solution.py:332
  (1 shorter events, 0.0 us)
Async XLA Ops:
  6.4 31.7 %all-to-all-start.1 = ((bf16[128,5,1,8,128]{4,3,1,2,0:T(8,128)(2,1)}), bf16[128,5,1,8,128]{4,3,1,2,0:T(8,128)(2,1)S(1)}, u32[]{:S(2)}, u32[]{:S(2)}) async-start(bf16[128,5,1,8,128]{4,3,1,2,0:T(8,128)(2,1)} %bitcast.14), calls=%async_computation.1 | async-start | bytes 2621440 | tf_op jit(solution)/shard_map/all_to_all | solution.py:357
  38.2 22.9 %copy-start = (bf16[128,5,1,8,128]{4,3,1,2,0:T(8,128)(2,1)}, bf16[128,5,1,8,128]{4,3,1,2,0:T(8,128)(2,1)S(1)}, u32[]{:S(2)}) copy-start(bf16[128,5,1,8,128]{4,3,1,2,0:T(8,128)(2,1)S(1)} %all-to-all-done.1) | copy-start | bytes 3932164
  38.2 69.2 %all-to-all-start = ((bf16[128,5,4,8,128]{4,3,2,1,0:T(8,128)(2,1)}), bf16[128,5,4,8,128]{4,3,2,1,0:T(8,128)(2,1)}, u32[]{:S(2)}, u32[]{:S(2)}) async-start(bf16[128,5,4,8,128]{4,3,2,1,0:T(8,128)(2,1)} %bitcast.15), calls=%async_computation | async-start | bytes 10485760 | tf_op jit(solution)/shard_map/all_to_all | solution.py:357

commit v6 on v5

--- a/solution.py
+++ b/solution.py
@@ -11,7 +11,7 @@
 F32 = jnp.float32
 BF16 = jnp.bfloat16
 AXES = ("grp", "band")
-CHUNKS = (1, 4)
+CHUNKS = (2, 3)
 
 
 def cos_sin_quarter(position, lon_count):

time: 178 us -> 180 us (1.011)
  transfers between devices with their start and end apart: 2 -> 2, of which waited for: 2 -> 2; matrix products, arithmetic and copies ran while one was open for 9% -> 9% of each run, Pallas kernels for 11% -> 10%
where the time goes in v6:
time: 180 us; the launch traced here: 179 us
  Pallas kernels  55.3 us (31%)
  waiting for transfers between devices  47 us (26%)
  blocking collectives  39.7 us (22%)
  starting transfers between devices  19.5 us (11%)
  local copies, waits for them, and re-layouts  16.6 us (9%)
    all_to_all x2, waiting for transfers between devices, exchange(): return lax.all_to_all(value, AXES, split_axis=0, concat_axis=0, tiled=True)  47 us
    all_to_all x2, blocking collectives, exchange(): return lax.all_to_all(value, AXES, split_axis=0, concat_axis=0, tiled=True)  39.7 us
    pallas_call x2, Pallas kernels, transform(): pl.pallas_call(functools.partial(fourier_kernel, chunk, pairs_total), in_...  19.5 us
    all_to_all x2, starting transfers between devices, exchange(): return lax.all_to_all(value, AXES, split_axis=0, concat_axis=0, tiled=True)  19.5 us
    pallas_call x1, Pallas kernels, finish(): pl.pallas_call(functools.partial(finish_kernel, 1.0 / total_rows), grid=(...  18.7 us
    pallas_call x2, Pallas kernels, project(): pl.pallas_call(functools.partial(legendre_kernel, later, last), grid=(pai...  17.1 us
    reshape x1, local copies, waits for them, and re-layouts, shards(): basis.transpose(0, 3, 1, 2).reshape(pairs, degree_rows, 2 * lat_total)  16.6 us
  transfers between devices with their start and end apart: 2, of which 2 were waited for; matrix products, arithmetic and copies ran while one was open for 9% of the time, Pallas kernels for 10%

profile of v6, /device:TPU:1, one launch (start us, length us, event | category | flops | bytes accessed | tf_op | source)
XLA Modules:
  0.0 179.1 jit_solution(4164868760536574819)
XLA Ops:
  0.6 8.3 %fourier.3 = bf16[2,64,5,2,8,128]{5,4,3,2,1,0:T(8,128)(2,1)} custom-call(s32[640]{0:T(1024)} %orders_ref.3, bf16[2,5,256,1280]{3,2,1,0:T(8,128)(2,1)} %bitcast.13), custom_call_target="tpu_custom_call" | custom-call | flops 3355443200 | bytes 9175040 | tf_op jit(solution)/shard_map/fourier/pallas_call | solution.py:114
  9.0 11.5 %all-to-all-start.1 = ((bf16[128,5,2,8,128]{4,3,2,1,0:T(8,128)(2,1)}), bf16[128,5,2,8,128]{4,3,2,1,0:T(8,128)(2,1)S(1)}, u32[]{:S(2)}, u32[]{:S(2)}) async-start(bf16[128,5,2,8,128]{4,3,2,1,0:T(8,128)(2,1)} %bitcast.12), calls=%async_computation.1 | async-start | bytes 5242880 | tf_op jit(solution)/shard_map/all_to_all | solution.py:357
  20.5 11.2 %fourier.2 = bf16[2,64,5,3,8,128]{5,4,3,2,1,0:T(8,128)(2,1)} custom-call(s32[640]{0:T(1024)} %orders_ref.3, bf16[2,5,256,1280]{3,2,1,0:T(8,128)(2,1)} %bitcast.14), custom_call_target="tpu_custom_call" | custom-call | flops 5033164800 | bytes 10485760 | tf_op jit(solution)/shard_map/fourier/pallas_call | solution.py:114
  31.7 22.9 %all-to-all-done.1 = bf16[128,5,2,8,128]{4,3,2,1,0:T(8,128)(2,1)S(1)} async-done(((bf16[128,5,2,8,128]{4,3,2,1,0:T(8,128)(2,1)}), bf16[128,5,2,8,128]{4,3,2,1,0:T(8,128)(2,1)S(1)}, u32[]{:S(2)}, u32[]{:S(2)}) %all-to-all-start.1) | async-done | bytes 2621472 | tf_op jit(solution)/shard_map/all_to_all | solution.py:357
  54.6 0.0 copy-start
  54.6 8.0 %all-to-all-start = ((bf16[128,5,3,8,128]{4,3,2,1,0:T(8,128)(2,1)}), bf16[128,5,3,8,128]{4,3,2,1,0:T(8,128)(2,1)}, u32[]{:S(2)}, u32[]{:S(2)}) async-start(bf16[128,5,3,8,128]{4,3,2,1,0:T(8,128)(2,1)} %bitcast.11), calls=%async_computation | async-start | bytes 7864320 | tf_op jit(solution)/shard_map/all_to_all | solution.py:357
  62.6 16.6 %reshape.22.basis_ref = bf16[5,641,1280]{2,1,0:T(8,128)(2,1)} reshape(bf16[5,641,2,640]{3,2,1,0:T(2,128)(2,1)} %bitcast.10) | data formatting | bytes 16409600 | tf_op jit(solution)/shard_map/reshape | solution.py:376
  79.2 0.0 copy-done
  79.2 7.4 %legendre.2 = (bf16[5,2,641,512]{3,2,1,0:T(8,128)(2,1)}, f32[256,256]{1,0:T(8,128)}) custom-call(bf16[640,2,8,128]{3,2,1,0:T(8,128)(2,1)} %bitcast.9, bf16[5,641,1280]{2,1,0:T(8,128)(2,1)} %reshape.22.basis_ref), custom_call_target="tpu_custom_call" | custom-call | flops 2688548864 | bytes 8528896 | tf_op jit(solution)/shard_map/legendre/pallas_call | solution.py:180
  86.6 24.0 %all-to-all-done = bf16[128,5,3,8,128]{4,3,2,1,0:T(8,128)(2,1)} async-done(((bf16[128,5,3,8,128]{4,3,2,1,0:T(8,128)(2,1)}), bf16[128,5,3,8,128]{4,3,2,1,0:T(8,128)(2,1)}, u32[]{:S(2)}, u32[]{:S(2)}) %all-to-all-start) | async-done | bytes 3932192 | tf_op jit(solution)/shard_map/all_to_all | solution.py:357
  110.6 9.7 %legendre.3 = (bf16[5,2,641,512]{3,2,1,0:T(8,128)(2,1)}, f32[128,4,128]{2,1,0:T(4,128)}) custom-call(bf16[640,3,8,128]{3,2,1,0:T(8,128)(2,1)} %bitcast.2.spectra_ref, bf16[5,641,1280]{2,1,0:T(8,128)(2,1)} %reshape.22.basis_ref, bf16[5,2,641,512]{3,2,1,0:T(8,128)(2,1)} %get-tuple-element.8.refs_0_, ...), custom_call_target="tpu_custom_call", output_to_operand_aliasing={{0}: (2, {})} | custom-call | flops 4032823296 | bytes 12793344 | tf_op jit(solution)/shard_map/legendre/pallas_call | solution.py:180
  120.3 24.5 %all_to_all.20 = f32[128,4,128]{2,1,0:T(4,128)S(1)} all-to-all(f32[128,4,128]{2,1,0:T(4,128)} %get-tuple-element.10), channel_id=1, replica_groups=mesh['grp'=2,'band'=64] {'grp','band'}, dimensions={0} | all-to-all | bytes 524288 | tf_op jit(solution)/shard_map/all_to_all | solution.py:357
  144.8 0.1 reduce_sum.9
  145.0 15.2 %all_to_all.21.pieces_ref = f32[128,4,128]{2,1,0:T(4,128)} all-to-all(f32[128,4,128]{2,1,0:T(4,128)S(1)} %broadcast_in_dim.4), channel_id=1, replica_groups=mesh['grp'=2,'band'=64] {'grp','band'}, dimensions={0} | all-to-all | bytes 524288 | tf_op jit(solution)/shard_map/all_to_all | solution.py:357
  160.3 18.7 %finish.1 = (bf16[5,641,2,256]{3,2,1,0:T(2,128)(2,1)}, f32[256,256]{1,0:T(8,128)}) custom-call(f32[128,4,128]{2,1,0:T(4,128)} %all_to_all.21.pieces_ref, bf16[5,2,641,512]{3,2,1,0:T(8,128)(2,1)} %get-tuple-element.11.part_any), custom_call_target="tpu_custom_call" | custom-call | tf_op jit(solution)/shard_map/finish/pallas_call | solution.py:332
  (1 shorter events, 0.0 us)
Async XLA Ops:
  9.0 45.7 %all-to-all-start.1 = ((bf16[128,5,2,8,128]{4,3,2,1,0:T(8,128)(2,1)}), bf16[128,5,2,8,128]{4,3,2,1,0:T(8,128)(2,1)S(1)}, u32[]{:S(2)}, u32[]{:S(2)}) async-start(bf16[128,5,2,8,128]{4,3,2,1,0:T(8,128)(2,1)} %bitcast.12), calls=%async_computation.1 | async-start | bytes 5242880 | tf_op jit(solution)/shard_map/all_to_all | solution.py:357
  54.6 24.6 %copy-start = (bf16[128,5,2,8,128]{4,3,2,1,0:T(8,128)(2,1)}, bf16[128,5,2,8,128]{4,3,2,1,0:T(8,128)(2,1)S(1)}, u32[]{:S(2)}) copy-start(bf16[128,5,2,8,128]{4,3,2,1,0:T(8,128)(2,1)S(1)} %all-to-all-done.1) | copy-start | bytes 7864324
  54.6 56.0 %all-to-all-start = ((bf16[128,5,3,8,128]{4,3,2,1,0:T(8,128)(2,1)}), bf16[128,5,3,8,128]{4,3,2,1,0:T(8,128)(2,1)}, u32[]{:S(2)}, u32[]{:S(2)}) async-start(bf16[128,5,3,8,128]{4,3,2,1,0:T(8,128)(2,1)} %bitcast.11), calls=%async_computation | async-start | bytes 7864320 | tf_op jit(solution)/shard_map/all_to_all | solution.py:357
